TPU v7x, 256 devices: a whole 4x4x8 slice. The times are simulated.
256 devices in a mesh: dp: 32 (over z, x), pipe: 2 (over core), tensor: 4 (over y).
Axes of the slice: x: 4, y: 4, z: 8, core: 2. Of those that a mesh axis runs over, the one named last changes fastest.
Arguments:
- tokens: bfloat16 [64, 64, 4096], P('dp', None, 'tensor'), may hold values from -8 to 8
- w_query: bfloat16 [2, 2, 4096, 4096], P(None, 'pipe', 'dp', 'tensor'), may hold values from -8 to 8
- w_key: bfloat16 [2, 2, 4096, 1024], P(None, 'pipe', 'dp', 'tensor'), may hold values from -1 to 1
- w_value: bfloat16 [2, 2, 4096, 1024], P(None, 'pipe', 'dp', 'tensor'), may hold values from -0.09375 to 0.09375
- w_out: bfloat16 [2, 2, 4096, 4096], P(None, 'pipe', 'tensor', 'dp'), may hold values from -0.09375 to 0.09375
- norm_gain: float32 [2, 2, 4096], P(None, 'pipe'), may hold values from 0.5 to 1.5
- boundary: int32 [64], P('dp'), may hold values from 1 to 63
- skip_offset: int32 [64], P('dp'), may hold values from 0 to 131008
- doc_lengths: int32 [64, 4], P('dp'), may hold values from 1 to 32, 64 in all within a row
- batch_order: int32 [32, 2], P('dp'), may hold values from 0 to 1, each once within a row
Outputs:
- final_state: bfloat16 [64, 64, 4096], P('dp', 'pipe', 'tensor')
Inputs may be any that keep to these rules, and one draw needn't show every extreme that they name: `doc_lengths`: each row sums to 64. `batch_order`: each row is a permutation.
All inputs are finite; a program needn't handle non-finite values.
Results may differ from a plain program's by a relative error of at most 0.014.
Values may be sent and summed in bfloat16 or wider, within the bound.
A program may use at most 192 MiB of HBM per device.

v0:
```python
from functools import partial

import jax
import jax.numpy as jnp
from jax import lax
from jax.sharding import PartitionSpec as P

HEAD_DIM = 128


ROPE_THETA = 500000.0
NORM_EPSILON = 1e-05


def cut_along(value, dim, peers):
    before, after = (value.shape[:dim], value.shape[dim + 1 :])
    return jnp.moveaxis(value.reshape(*before, peers, -1, *after), dim, 0)


def sent_and_summed(value, axis, dim):
    peers = lax.axis_size(axis)
    blocks = lax.all_to_all(cut_along(value, dim, peers), axis, 0, 0, tiled=True)
    return jnp.sum(blocks, axis=0)


def sent_together(arrays, axis, dim, along):
    widths = [a.shape[along] for a in arrays]
    both = jnp.concatenate(arrays, axis=along)
    whole = lax.all_gather(both, axis, axis=dim, tiled=True)
    return tuple(jnp.split(whole, [sum(widths[:k]) for k in range(1, len(widths))], axis=along))


def from_behind(value, axis, by):
    peers = lax.axis_size(axis)
    pairs = [(i, i + by) for i in range(peers) if 0 <= i + by < peers]
    return lax.ppermute(value, axis, pairs)


def picked(value, axis, root):
    return lax.dynamic_index_in_dim(lax.all_gather(value, axis), root, 0, keepdims=False)


def rope_angles(positions, head_dim):
    half_dim = head_dim // 2
    exponent = jnp.arange(half_dim, dtype=jnp.float32) * (2.0 / head_dim)
    frequency = jnp.float32(ROPE_THETA) ** (-exponent)
    return positions.astype(jnp.float32)[..., None] * frequency


def rotate(values, angles):
    half_dim = values.shape[-1] // 2
    first_half = values[..., :half_dim]
    second = values[..., half_dim:]
    cosine = jnp.cos(angles)[:, None, :]
    sine_part = jnp.sin(angles)[:, None, :]
    return jnp.concatenate(
        [first_half * cosine - second * sine_part, second * cosine + first_half * sine_part],
        axis=-1,
    )


def sample_layout(first_cut, offset, lengths, seq_len):
    places = jnp.arange(seq_len, dtype=jnp.int32)
    positions = jnp.where(places < first_cut, places, places + offset)
    doc_ends = jnp.cumsum(lengths)
    doc_ids = jnp.sum((places[:, None] >= doc_ends[None, :]).astype(jnp.int32), axis=1)
    allowed = (doc_ids[:, None] == doc_ids[None, :]) & (places[None, :] <= places[:, None])
    return (positions, allowed)


def attend(normed, q_weight, k_weight, v_weight, angles, allowed):
    seq_len = normed.shape[0]
    q_heads = q_weight.shape[1] // HEAD_DIM
    kv_heads = k_weight.shape[1] // HEAD_DIM
    group_size = q_heads // kv_heads
    queries = jnp.dot(normed, q_weight, preferred_element_type=jnp.float32)
    key_vecs = jnp.dot(normed, k_weight, preferred_element_type=jnp.float32)
    value_vecs = jnp.dot(normed, v_weight, preferred_element_type=jnp.float32).astype(jnp.bfloat16)
    value_vecs = value_vecs.reshape(seq_len, kv_heads, HEAD_DIM)
    queries = rotate(queries.reshape(seq_len, q_heads, HEAD_DIM), angles).astype(jnp.bfloat16)
    queries = queries.reshape(seq_len, kv_heads, group_size, HEAD_DIM)
    key_vecs = rotate(key_vecs.reshape(seq_len, kv_heads, HEAD_DIM), angles).astype(jnp.bfloat16)
    scores = jnp.einsum(
        "skgd,tkd->kgst", queries, key_vecs, preferred_element_type=jnp.float32
    ) * HEAD_DIM ** (-0.5)
    scores = jnp.where(allowed[None, None], scores, -jnp.inf)
    row_max = jnp.max(scores, axis=-1, keepdims=True)
    exp_scores = jnp.exp(scores - row_max)
    weights = (exp_scores / jnp.sum(exp_scores, axis=-1, keepdims=True)).astype(jnp.bfloat16)
    mixed = jnp.einsum("kgst,tkd->skgd", weights, value_vecs, preferred_element_type=jnp.float32)
    return mixed.reshape(seq_len, q_heads * HEAD_DIM)


def layer_step(stream, active, gain_row, weight_three, out_part, angles, allowed):
    gathered = lax.all_gather(stream, "tensor", axis=1, tiled=True)
    seq_len = gathered.shape[0]
    head_width = weight_three[0].shape[1]

    def local_mix():
        widened = gathered.astype(jnp.float32)
        inv_rms = lax.rsqrt(jnp.mean(widened * widened, axis=-1, keepdims=True) + NORM_EPSILON)
        normed = (widened * inv_rms * gain_row).astype(jnp.bfloat16)
        return attend(
            normed, weight_three[0], weight_three[1], weight_three[2], angles, allowed
        ).astype(jnp.bfloat16)

    mixed = lax.cond(active, local_mix, lambda: jnp.zeros((seq_len, head_width), jnp.bfloat16))
    partial_sum = lax.cond(
        active,
        lambda: jnp.dot(mixed, out_part, preferred_element_type=jnp.float32),
        lambda: jnp.zeros((mixed.shape[0], out_part.shape[1]), jnp.float32),
    )
    shares = sent_and_summed(partial_sum, "tensor", 1)
    updated = (stream.astype(jnp.float32) + shares).astype(jnp.bfloat16)
    return jnp.where(active, updated, jnp.zeros_like(updated))


def per_device(
    tokens,
    w_query,
    w_key,
    w_value,
    w_out,
    norm_gain,
    boundary,
    skip_offset,
    doc_lengths,
    batch_order,
):
    sections = lax.axis_size("pipe")
    my_section = lax.axis_index("pipe")
    micro_count = tokens.shape[0]
    seq_len = tokens.shape[1]
    local_width = tokens.shape[2]
    ordered = batch_order[0]
    doc_costs = jnp.sum(doc_lengths * doc_lengths, axis=1)
    slot_cost = jnp.take(doc_costs, ordered)
    slot_of = jnp.argsort(-slot_cost, stable=True)
    samples = jnp.take(ordered, slot_of)
    feed_rows = jnp.take(tokens, samples, axis=0)
    positions, allowed = jax.vmap(partial(sample_layout, seq_len=seq_len))(
        jnp.take(boundary, samples),
        jnp.take(skip_offset, samples),
        jnp.take(doc_lengths, samples, axis=0),
    )
    angles = rope_angles(positions, HEAD_DIM)
    down_gain = norm_gain[0, 0]
    up_gain = norm_gain[1, 0]
    out_full = lax.all_gather(w_out, "dp", axis=3, tiled=True)
    down_out_part = out_full[0, 0]
    up_out_part = out_full[1, 0]
    query_full, key_full, value_full = sent_together((w_query, w_key, w_value), "dp", 2, 3)
    down_three = (query_full[0, 0], key_full[0, 0], value_full[0, 0])
    up_three = (query_full[1, 0], key_full[1, 0], value_full[1, 0])
    step_count = micro_count + 2 * sections - 2
    empty_rows = jnp.zeros((seq_len, local_width), jnp.bfloat16)
    last_item = micro_count - 1

    def select_item(stacked, item_index):
        return lax.dynamic_index_in_dim(
            stacked, jnp.clip(item_index, 0, last_item), 0, keepdims=False
        )

    def advance(tick_now, loop_state):
        down_buf, up_buf, results, up_weights = loop_state
        down_item = tick_now - my_section
        down_ok = (down_item >= 0) & (down_item < micro_count)
        down_in = jnp.where(my_section == 0, select_item(feed_rows, tick_now), down_buf)
        down_out = layer_step(
            down_in,
            down_ok,
            down_gain,
            down_three,
            down_out_part,
            select_item(angles, down_item),
            select_item(allowed, down_item),
        )
        up_item = tick_now - (2 * sections - 2 - my_section)
        up_ok = (up_item >= 0) & (up_item < micro_count)
        up_in = jnp.where(my_section == sections - 1, down_out, up_buf)
        up_out = layer_step(
            up_in,
            up_ok,
            up_gain,
            up_weights,
            up_out_part,
            select_item(angles, up_item),
            select_item(allowed, up_item),
        )
        out_slot = select_item(slot_of, up_item)
        stored = lax.dynamic_update_index_in_dim(results, up_out, out_slot, 0)
        results = jnp.where(up_ok & (my_section == 0), stored, results)
        down_buf = from_behind(down_out, "pipe", 1)
        up_buf = from_behind(up_out, "pipe", -1)
        return (down_buf, up_buf, results, up_weights)

    initial = (
        empty_rows,
        empty_rows,
        jnp.zeros((micro_count, seq_len, local_width), jnp.bfloat16),
        up_three,
    )
    down_buf, up_buf, results, up_weights = lax.fori_loop(0, step_count, advance, initial)
    spread = picked(results, "pipe", 0)
    row_count = seq_len // sections
    return lax.dynamic_slice_in_dim(spread, my_section * row_count, row_count, 1)


def solution(mesh):
    placed = (
        P("dp", None, "tensor"),
        P(None, "pipe", "dp", "tensor"),
        P(None, "pipe", "dp", "tensor"),
        P(None, "pipe", "dp", "tensor"),
        P(None, "pipe", "tensor", "dp"),
        P(None, "pipe", None),
        P("dp"),
        P("dp"),
        P("dp", None),
        P("dp", None),
    )
    return jax.shard_map(
        per_device, mesh=mesh, in_specs=placed, out_specs=P("dp", "pipe", "tensor"), check_vma=False
    )
```

profile of v0, /device:TPU:1, one launch (start us, length us, event | category | flops | bytes accessed | tf_op | source)
XLA Modules:
  0.0 725.0 jit_solution(7644802526432635606)
XLA Ops:
  7.3 2.1 pad_maximum_fusion
  22.8 136.4 %all-gather.6.cloned.1.call-done = bf16[2,1,1024,4096]{3,2,1,0:T(8,128)(2,1)} async-done(((bf16[2,1,1024,128]{3,2,1,0:T(8,128)(2,1)}), bf16[2,1,1024,4096]{3,2,1,0:T(8,128)(2,1)}) %all-gather.6.cloned.1.call-update) | async-done | bytes 16777232 | tf_op jit(solution)/shard_map/all_gather | solution.py:149
  159.2 11.7 %slice_bitcast_fusion = (bf16[1024,4096]{1,0:T(8,128)(2,1)}, bf16[1024,4096]{1,0:T(8,128)(2,1)}) fusion(bf16[2,1,1024,4096]{3,2,1,0:T(8,128)(2,1)} %all-gather.6.cloned.1.call-done), kind=kLoop, calls=%fused_computation.98 | loop fusion | bytes 33554432 | tf_op jit(solution)/shard_map/squeeze | solution.py:151
  170.9 174.1 %all-gather.4.cloned.1.call-done = bf16[2,1,4096,1536]{3,2,1,0:T(8,128)(2,1)} async-done(((bf16[2,1,128,1536]{3,2,1,0:T(8,128)(2,1)}), bf16[2,1,4096,1536]{3,2,1,0:T(8,128)(2,1)}) %all-gather.4.cloned.1.call-update) | async-done | bytes 25165840 | tf_op jit(solution)/shard_map/all_gather | solution.py:29
  345.0 6.3 slice_bitcast_fusion.4
  351.3 11.6 %slice_bitcast_fusion.1 = (bf16[4096,1024]{1,0:T(8,128)(2,1)}, bf16[4096,1024]{1,0:T(8,128)(2,1)}) fusion(bf16[2,1,4096,1536]{3,2,1,0:T(8,128)(2,1)} %all-gather.4.cloned.1.call-done), kind=kLoop, calls=%fused_computation.99 | loop fusion | bytes 33554432 | tf_op jit(solution)/shard_map/squeeze | solution.py:154
  363.6 351.6 %while.19 = (s32[]{:T(128)}, bf16[64,1024]{1,0:T(8,128)(2,1)}, bf16[64,1024]{1,0:T(8,128)(2,1)S(1)}, bf16[2,64,1024]{2,1,0:T(8,128)(2,1)S(1)}, s32[]{:T(128)}, /...) while((s32[]{:T(128)}, bf16[64,1024]{1,0:T(8,128)(2,1)}, ...), condition=%wide.region_21.23_spmd.clone, body=%wide.region_4.22_spmd.clone.sunk | while | flops 2746410496 | bytes 85502200 | solution.py:203
  364.6 11.5 %all_gather.36 = bf16[64,4096]{1,0:T(8,128)(2,1)S(1)} all-gather(bf16[64,1024]{1,0:T(8,128)(2,1)S(1)} %bitcast_select_fusion.3), channel_id=1, replica_groups=mesh['dp'=32,'pipe'=2,'tensor'=4] {'tensor'}, dimensions={1}, use_global_device_ids=true | all-gather | bytes 655360 | tf_op jit(solution)/shard_map/while/body/eval_jaxpr/all_gather | solution.py:95
  378.5 1.6 copy.113
  380.1 3.5 all-to-all-start
  383.7 9.7 %all-to-all-done = f32[4,64,1024]{2,1,0:T(8,128)S(1)} async-done(((f32[4,64,1024]{2,1,0:T(8,128)}), f32[4,64,1024]{2,1,0:T(8,128)S(1)}, u32[]{:S(2)}, u32[]{:S(2)}) %all-to-all-start) | async-done | bytes 1048608 | tf_op jit(solution)/shard_map/while/body/eval_jaxpr/all_to_all | solution.py:22
  394.2 9.9 %all_gather.37 = bf16[64,4096]{1,0:T(8,128)(2,1)S(1)} all-gather(bf16[64,1024]{1,0:T(8,128)(2,1)S(1)} %get-tuple-element.869), channel_id=1, replica_groups=mesh['dp'=32,'pipe'=2,'tensor'=4] {'tensor'}, dimensions={1}, use_global_device_ids=true | all-gather | bytes 655360 | tf_op jit(solution)/shard_map/while/body/eval_jaxpr/all_gather | solution.py:95
  404.9 1.6 copy.114
  406.5 3.5 all-to-all-start.1
  413.6 6.4 all-to-all-done.1
  420.2 26.8 %collective-permute-start.1 = (bf16[64,1024]{1,0:T(8,128)(2,1)S(1)}, bf16[64,1024]{1,0:T(8,128)(2,1)S(1)}, u32[]{:S(2)}, u32[]{:S(2)}) collective-permute-start(bf16[64,1024]{1,0:T(8,128)(2,1)S(1)} %get-tuple-element.870), channel_id=1, source_target_pairs={{4,0},{5,1},{6,2},{7,3},{12,8},{13,9},{14,10},{15,11},{20,16},{21,... | collective-permute-start | bytes 393224 | tf_op jit(solution)/shard_map/while/body/eval_jaxpr/ppermute | solution.py:36
  448.9 9.9 %all_gather.36 = bf16[64,4096]{1,0:T(8,128)(2,1)S(1)} all-gather(bf16[64,1024]{1,0:T(8,128)(2,1)S(1)} %bitcast_select_fusion.3), channel_id=1, replica_groups=mesh['dp'=32,'pipe'=2,'tensor'=4] {'tensor'}, dimensions={1}, use_global_device_ids=true | all-gather | bytes 655360 | tf_op jit(solution)/shard_map/while/body/eval_jaxpr/all_gather | solution.py:95
  460.4 11.3 %conditional.12 = (bf16[64,1024]{1,0:T(8,128)(2,1)S(1)}) conditional(s32[]{:T(128)} %convert_element_type.206, () %tuple.107, (bf16[64,4096]{1,0:T(8,128)(2,1)S(1)}, f32[1,1,4096]{2,1,0:T(1,128)S(1)}, bf16[4096,256]{1,0:T(8,128)(2,1)}, s32[]{:T(128)}, pred[2,64,64]{1,2,0:T(8,128)(4,1)S(1)}, /*index=5*/bf16[4096,256]{1,0:T(8,128)(2,1)}, ...), branch_computations={%region_5.6_spmd, %region_6.10_spmd} | conditional | flops 835764928 | bytes 17847848 | solution.py:107
  460.7 2.1 fusion.41
  463.2 5.0 convolution_bitcast_fusion
  468.8 2.1 convolution_convert_fusion.1
  471.7 5.0 conditional.13
  471.8 4.9 fusion.100
  477.4 1.6 copy.113
  479.0 3.5 all-to-all-start
  482.6 11.3 %all-to-all-done = f32[4,64,1024]{2,1,0:T(8,128)S(1)} async-done(((f32[4,64,1024]{2,1,0:T(8,128)}), f32[4,64,1024]{2,1,0:T(8,128)S(1)}, u32[]{:S(2)}, u32[]{:S(2)}) %all-to-all-start) | async-done | bytes 1048608 | tf_op jit(solution)/shard_map/while/body/eval_jaxpr/all_to_all | solution.py:22
  494.7 10.7 %all_gather.37 = bf16[64,4096]{1,0:T(8,128)(2,1)S(1)} all-gather(bf16[64,1024]{1,0:T(8,128)(2,1)S(1)} %get-tuple-element.869), channel_id=1, replica_groups=mesh['dp'=32,'pipe'=2,'tensor'=4] {'tensor'}, dimensions={1}, use_global_device_ids=true | all-gather | bytes 655360 | tf_op jit(solution)/shard_map/while/body/eval_jaxpr/all_gather | solution.py:95
  505.4 11.5 %conditional.14 = (bf16[64,1024]{1,0:T(8,128)(2,1)S(1)}) conditional(s32[]{:T(128)} %convert_element_type.207, () %tuple.111, (bf16[64,4096]{1,0:T(8,128)(2,1)S(1)}, f32[1,1,4096]{2,1,0:T(1,128)S(1)}, bf16[4096,256]{1,0:T(8,128)(2,1)}, pred[2,64,64]{1,2,0:T(8,128)(4,1)S(1)}, s32[]{:T(128)}, /*index=5*/bf16[4096,256]{1,0:T(8,128)(2,1)}, ...), branch_computations={%region_13.14_spmd, %region_14.18_spmd} | conditional | flops 835764928 | bytes 26319488 | solution.py:107
  505.6 2.1 fusion.81
  508.1 5.2 convolution_bitcast_fusion.1
  516.9 5.0 conditional.15
  517.0 5.0 fusion.101
  522.7 1.6 copy.114
  524.3 3.5 all-to-all-start.1
  531.4 6.1 all-to-all-done.1
  540.9 9.9 %all_gather.36 = bf16[64,4096]{1,0:T(8,128)(2,1)S(1)} all-gather(bf16[64,1024]{1,0:T(8,128)(2,1)S(1)} %bitcast_select_fusion.3), channel_id=1, replica_groups=mesh['dp'=32,'pipe'=2,'tensor'=4] {'tensor'}, dimensions={1}, use_global_device_ids=true | all-gather | bytes 655360 | tf_op jit(solution)/shard_map/while/body/eval_jaxpr/all_gather | solution.py:95
  552.4 11.3 %conditional.12 = (bf16[64,1024]{1,0:T(8,128)(2,1)S(1)}) conditional(s32[]{:T(128)} %convert_element_type.206, () %tuple.107, (bf16[64,4096]{1,0:T(8,128)(2,1)S(1)}, f32[1,1,4096]{2,1,0:T(1,128)S(1)}, bf16[4096,256]{1,0:T(8,128)(2,1)}, s32[]{:T(128)}, pred[2,64,64]{1,2,0:T(8,128)(4,1)S(1)}, /*index=5*/bf16[4096,256]{1,0:T(8,128)(2,1)}, ...), branch_computations={%region_5.6_spmd, %region_6.10_spmd} | conditional | flops 835764928 | bytes 17847848 | solution.py:107
  552.6 2.1 fusion.41
  555.1 5.0 convolution_bitcast_fusion
  560.8 2.1 convolution_convert_fusion.1
  563.7 5.0 conditional.13
  563.7 4.9 fusion.100
  569.4 1.6 copy.113
  571.0 3.5 all-to-all-start
  574.5 10.6 %all-to-all-done = f32[4,64,1024]{2,1,0:T(8,128)S(1)} async-done(((f32[4,64,1024]{2,1,0:T(8,128)}), f32[4,64,1024]{2,1,0:T(8,128)S(1)}, u32[]{:S(2)}, u32[]{:S(2)}) %all-to-all-start) | async-done | bytes 1048608 | tf_op jit(solution)/shard_map/while/body/eval_jaxpr/all_to_all | solution.py:22
  586.0 9.9 %all_gather.37 = bf16[64,4096]{1,0:T(8,128)(2,1)S(1)} all-gather(bf16[64,1024]{1,0:T(8,128)(2,1)S(1)} %get-tuple-element.869), channel_id=1, replica_groups=mesh['dp'=32,'pipe'=2,'tensor'=4] {'tensor'}, dimensions={1}, use_global_device_ids=true | all-gather | bytes 655360 | tf_op jit(solution)/shard_map/while/body/eval_jaxpr/all_gather | solution.py:95
  595.8 11.5 %conditional.14 = (bf16[64,1024]{1,0:T(8,128)(2,1)S(1)}) conditional(s32[]{:T(128)} %convert_element_type.207, () %tuple.111, (bf16[64,4096]{1,0:T(8,128)(2,1)S(1)}, f32[1,1,4096]{2,1,0:T(1,128)S(1)}, bf16[4096,256]{1,0:T(8,128)(2,1)}, pred[2,64,64]{1,2,0:T(8,128)(4,1)S(1)}, s32[]{:T(128)}, /*index=5*/bf16[4096,256]{1,0:T(8,128)(2,1)}, ...), branch_computations={%region_13.14_spmd, %region_14.18_spmd} | conditional | flops 835764928 | bytes 26319488 | solution.py:107
  596.1 2.1 fusion.81
  598.6 5.1 convolution_bitcast_fusion.1
  607.4 5.0 conditional.15
  607.4 5.0 fusion.101
  613.1 1.6 copy.114
  614.7 3.5 all-to-all-start.1
  621.8 6.1 all-to-all-done.1
  631.4 9.9 %all_gather.36 = bf16[64,4096]{1,0:T(8,128)(2,1)S(1)} all-gather(bf16[64,1024]{1,0:T(8,128)(2,1)S(1)} %bitcast_select_fusion.3), channel_id=1, replica_groups=mesh['dp'=32,'pipe'=2,'tensor'=4] {'tensor'}, dimensions={1}, use_global_device_ids=true | all-gather | bytes 655360 | tf_op jit(solution)/shard_map/while/body/eval_jaxpr/all_gather | solution.py:95
  643.7 1.6 copy.113
  645.3 3.5 all-to-all-start
  648.8 11.3 %all-to-all-done = f32[4,64,1024]{2,1,0:T(8,128)S(1)} async-done(((f32[4,64,1024]{2,1,0:T(8,128)}), f32[4,64,1024]{2,1,0:T(8,128)S(1)}, u32[]{:S(2)}, u32[]{:S(2)}) %all-to-all-start) | async-done | bytes 1048608 | tf_op jit(solution)/shard_map/while/body/eval_jaxpr/all_to_all | solution.py:22
  661.0 10.7 %all_gather.37 = bf16[64,4096]{1,0:T(8,128)(2,1)S(1)} all-gather(bf16[64,1024]{1,0:T(8,128)(2,1)S(1)} %get-tuple-element.869), channel_id=1, replica_groups=mesh['dp'=32,'pipe'=2,'tensor'=4] {'tensor'}, dimensions={1}, use_global_device_ids=true | all-gather | bytes 655360 | tf_op jit(solution)/shard_map/while/body/eval_jaxpr/all_gather | solution.py:95
  672.5 1.6 copy.114
  674.1 3.5 all-to-all-start.1
  681.2 6.1 all-to-all-done.1
  687.5 26.7 %collective-permute-start.1 = (bf16[64,1024]{1,0:T(8,128)(2,1)S(1)}, bf16[64,1024]{1,0:T(8,128)(2,1)S(1)}, u32[]{:S(2)}, u32[]{:S(2)}) collective-permute-start(bf16[64,1024]{1,0:T(8,128)(2,1)S(1)} %get-tuple-element.870), channel_id=1, source_target_pairs={{4,0},{5,1},{6,2},{7,3},{12,8},{13,9},{14,10},{15,11},{20,16},{21,... | collective-permute-start | bytes 393224 | tf_op jit(solution)/shard_map/while/body/eval_jaxpr/ppermute | solution.py:36
  715.2 2.3 all-gather
  (208 shorter events, 61.9 us)
Async XLA Ops:
  6.5 11.5 %copy-start = (bf16[2,64,1024]{2,1,0:T(8,128)(2,1)S(1)}, bf16[2,64,1024]{2,1,0:T(8,128)(2,1)}, u32[]{:S(2)}) copy-start(bf16[2,64,1024]{2,1,0:T(8,128)(2,1)} %param.22) | copy-start | bytes 786436
  6.5 152.7 %all-gather.6.cloned.1.call-start = ((), (), s32[]{:S(2)}) async-start(), calls=%async_computation.3 | async-start | bytes 17301504 | tf_op jit(solution)/shard_map/all_gather | solution.py:149
  7.3 337.8 %all-gather.4.cloned.1.call-start = ((), (), s32[]{:S(2)}) async-start(), calls=%async_computation.2 | async-start | bytes 25952256 | tf_op jit(solution)/shard_map/all_gather | solution.py:29
  12.8 3.9 copy-start.7
  380.1 13.2 %all-to-all-start = ((f32[4,64,1024]{2,1,0:T(8,128)}), f32[4,64,1024]{2,1,0:T(8,128)S(1)}, u32[]{:S(2)}, u32[]{:S(2)}) async-start(f32[4,64,1024]{2,1,0:T(8,128)} %copy.113), calls=%async_computation | async-start | bytes 2097152 | tf_op jit(solution)/shard_map/while/body/eval_jaxpr/all_to_all | solution.py:22
  404.1 6.0 copy-start.8
  404.1 8.2 %copy-start.3 = (bf16[64,1024]{1,0:T(8,128)(2,1)S(1)}, bf16[64,1024]{1,0:T(8,128)(2,1)}, u32[]{:S(2)}) copy-start(bf16[64,1024]{1,0:T(8,128)(2,1)} %get-tuple-element.868) | copy-start | bytes 393220 | tf_op jit(solution)/shard_map/while
  406.5 13.5 %all-to-all-start.1 = ((f32[4,64,1024]{2,1,0:T(8,128)}), f32[4,64,1024]{2,1,0:T(8,128)S(1)}, u32[]{:S(2)}, u32[]{:S(2)}) async-start(f32[4,64,1024]{2,1,0:T(8,128)} %copy.114), calls=%async_computation.1 | async-start | bytes 2097152 | tf_op jit(solution)/shard_map/while/body/eval_jaxpr/all_to_all | solution.py:22
  412.3 34.6 %collective-permute-start = (bf16[64,1024]{1,0:T(8,128)(2,1)S(1)}, bf16[64,1024]{1,0:T(8,128)(2,1)}, u32[]{:S(2)}, u32[]{:S(2)}) collective-permute-start(bf16[64,1024]{1,0:T(8,128)(2,1)S(1)} %copy-done.3), channel_id=1, source_target_pairs={{0,4},{1,5},{2,6},{3,7},{8,12},{9,13},{10,14},{11,15},{16,20},{17,... | collective-permute-start | bytes 393224 | tf_op jit(solution)/shard_map/while/body/eval_jaxpr/ppermute | solution.py:36
  420.2 27.7 %collective-permute-start.1 = (bf16[64,1024]{1,0:T(8,128)(2,1)S(1)}, bf16[64,1024]{1,0:T(8,128)(2,1)S(1)}, u32[]{:S(2)}, u32[]{:S(2)}) collective-permute-start(bf16[64,1024]{1,0:T(8,128)(2,1)S(1)} %get-tuple-element.870), channel_id=1, source_target_pairs={{4,0},{5,1},{6,2},{7,3},{12,8},{13,9},{14,10},{15,11},{20,16},{21,... | collective-permute-start | bytes 393224 | tf_op jit(solution)/shard_map/while/body/eval_jaxpr/ppermute | solution.py:36
  479.0 14.9 %all-to-all-start = ((f32[4,64,1024]{2,1,0:T(8,128)}), f32[4,64,1024]{2,1,0:T(8,128)S(1)}, u32[]{:S(2)}, u32[]{:S(2)}) async-start(f32[4,64,1024]{2,1,0:T(8,128)} %copy.113), calls=%async_computation | async-start | bytes 2097152 | tf_op jit(solution)/shard_map/while/body/eval_jaxpr/all_to_all | solution.py:22
  505.6 2.5 copy-start.5
  508.1 5.5 copy-start.4
  508.1 6.1 copy-start.2
  513.6 0.6 copy-start.6
  516.9 10.9 %copy-start.8 = (s32[2]{0:T(128)S(1)}, s32[2]{0:T(128)}, u32[]{:S(2)}) copy-start(s32[2]{0:T(128)} %get-tuple-element.947) | copy-start | bytes 28 | tf_op jit(solution)/shard_map/while
  516.9 13.2 %copy-start.3 = (bf16[64,1024]{1,0:T(8,128)(2,1)S(1)}, bf16[64,1024]{1,0:T(8,128)(2,1)}, u32[]{:S(2)}) copy-start(bf16[64,1024]{1,0:T(8,128)(2,1)} %get-tuple-element.868) | copy-start | bytes 393220 | tf_op jit(solution)/shard_map/while
  524.3 13.2 %all-to-all-start.1 = ((f32[4,64,1024]{2,1,0:T(8,128)}), f32[4,64,1024]{2,1,0:T(8,128)S(1)}, u32[]{:S(2)}, u32[]{:S(2)}) async-start(f32[4,64,1024]{2,1,0:T(8,128)} %copy.114), calls=%async_computation.1 | async-start | bytes 2097152 | tf_op jit(solution)/shard_map/while/body/eval_jaxpr/all_to_all | solution.py:22
  530.1 8.9 %collective-permute-start = (bf16[64,1024]{1,0:T(8,128)(2,1)S(1)}, bf16[64,1024]{1,0:T(8,128)(2,1)}, u32[]{:S(2)}, u32[]{:S(2)}) collective-permute-start(bf16[64,1024]{1,0:T(8,128)(2,1)S(1)} %copy-done.3), channel_id=1, source_target_pairs={{0,4},{1,5},{2,6},{3,7},{8,12},{9,13},{10,14},{11,15},{16,20},{17,... | collective-permute-start | bytes 393224 | tf_op jit(solution)/shard_map/while/body/eval_jaxpr/ppermute | solution.py:36
  537.6 2.3 collective-permute-start.1
  571.0 14.2 %all-to-all-start = ((f32[4,64,1024]{2,1,0:T(8,128)}), f32[4,64,1024]{2,1,0:T(8,128)S(1)}, u32[]{:S(2)}, u32[]{:S(2)}) async-start(f32[4,64,1024]{2,1,0:T(8,128)} %copy.113), calls=%async_computation | async-start | bytes 2097152 | tf_op jit(solution)/shard_map/while/body/eval_jaxpr/all_to_all | solution.py:22
  596.1 2.5 copy-start.5
  598.5 5.5 copy-start.4
  598.6 6.1 copy-start.2
  604.0 0.6 copy-start.6
  607.4 10.9 %copy-start.8 = (s32[2]{0:T(128)S(1)}, s32[2]{0:T(128)}, u32[]{:S(2)}) copy-start(s32[2]{0:T(128)} %get-tuple-element.947) | copy-start | bytes 28 | tf_op jit(solution)/shard_map/while
  607.4 13.2 %copy-start.3 = (bf16[64,1024]{1,0:T(8,128)(2,1)S(1)}, bf16[64,1024]{1,0:T(8,128)(2,1)}, u32[]{:S(2)}) copy-start(bf16[64,1024]{1,0:T(8,128)(2,1)} %get-tuple-element.868) | copy-start | bytes 393220 | tf_op jit(solution)/shard_map/while
  614.7 13.2 %all-to-all-start.1 = ((f32[4,64,1024]{2,1,0:T(8,128)}), f32[4,64,1024]{2,1,0:T(8,128)S(1)}, u32[]{:S(2)}, u32[]{:S(2)}) async-start(f32[4,64,1024]{2,1,0:T(8,128)} %copy.114), calls=%async_computation.1 | async-start | bytes 2097152 | tf_op jit(solution)/shard_map/while/body/eval_jaxpr/all_to_all | solution.py:22
  620.5 8.9 %collective-permute-start = (bf16[64,1024]{1,0:T(8,128)(2,1)S(1)}, bf16[64,1024]{1,0:T(8,128)(2,1)}, u32[]{:S(2)}, u32[]{:S(2)}) collective-permute-start(bf16[64,1024]{1,0:T(8,128)(2,1)S(1)} %copy-done.3), channel_id=1, source_target_pairs={{0,4},{1,5},{2,6},{3,7},{8,12},{9,13},{10,14},{11,15},{16,20},{17,... | collective-permute-start | bytes 393224 | tf_op jit(solution)/shard_map/while/body/eval_jaxpr/ppermute | solution.py:36
  628.1 2.3 collective-permute-start.1
  645.3 14.9 %all-to-all-start = ((f32[4,64,1024]{2,1,0:T(8,128)}), f32[4,64,1024]{2,1,0:T(8,128)S(1)}, u32[]{:S(2)}, u32[]{:S(2)}) async-start(f32[4,64,1024]{2,1,0:T(8,128)} %copy.113), calls=%async_computation | async-start | bytes 2097152 | tf_op jit(solution)/shard_map/while/body/eval_jaxpr/all_to_all | solution.py:22
  671.7 6.0 copy-start.8
  671.7 8.2 %copy-start.3 = (bf16[64,1024]{1,0:T(8,128)(2,1)S(1)}, bf16[64,1024]{1,0:T(8,128)(2,1)}, u32[]{:S(2)}) copy-start(bf16[64,1024]{1,0:T(8,128)(2,1)} %get-tuple-element.868) | copy-start | bytes 393220 | tf_op jit(solution)/shard_map/while
  674.1 13.2 %all-to-all-start.1 = ((f32[4,64,1024]{2,1,0:T(8,128)}), f32[4,64,1024]{2,1,0:T(8,128)S(1)}, u32[]{:S(2)}, u32[]{:S(2)}) async-start(f32[4,64,1024]{2,1,0:T(8,128)} %copy.114), calls=%async_computation.1 | async-start | bytes 2097152 | tf_op jit(solution)/shard_map/while/body/eval_jaxpr/all_to_all | solution.py:22
  679.9 34.3 %collective-permute-start = (bf16[64,1024]{1,0:T(8,128)(2,1)S(1)}, bf16[64,1024]{1,0:T(8,128)(2,1)}, u32[]{:S(2)}, u32[]{:S(2)}) collective-permute-start(bf16[64,1024]{1,0:T(8,128)(2,1)S(1)} %copy-done.3), channel_id=1, source_target_pairs={{0,4},{1,5},{2,6},{3,7},{8,12},{9,13},{10,14},{11,15},{16,20},{17,... | collective-permute-start | bytes 393224 | tf_op jit(solution)/shard_map/while/body/eval_jaxpr/ppermute | solution.py:36
  687.5 27.7 %collective-permute-start.1 = (bf16[64,1024]{1,0:T(8,128)(2,1)S(1)}, bf16[64,1024]{1,0:T(8,128)(2,1)S(1)}, u32[]{:S(2)}, u32[]{:S(2)}) collective-permute-start(bf16[64,1024]{1,0:T(8,128)(2,1)S(1)} %get-tuple-element.870), channel_id=1, source_target_pairs={{4,0},{5,1},{6,2},{7,3},{12,8},{13,9},{14,10},{15,11},{20,16},{21,... | collective-permute-start | bytes 393224 | tf_op jit(solution)/shard_map/while/body/eval_jaxpr/ppermute | solution.py:36
  715.2 3.0 copy-start.1
Sparse Core Ops, SparseCore 0:
  9.8 149.3 all-gather.5
  161.8 183.1 all-gather.3
where the time goes:
time: 727 us; the launch traced here: 725 us
  waiting for transfers between devices  383 us (53%)
  starting transfers between devices  89.4 us (12%)
  blocking collectives  84.6 us (12%)
  local copies, waits for them, and re-layouts  62.1 us (9%)
  matrix products  60.5 us (8%)
  other arithmetic  24 us (3%)
  between operations  13.5 us (2%)
  loops' own time  8.27 us (1%)
    all_gather x1, waiting for transfers between devices, sent_together(): whole = lax.all_gather(both, axis, axis=dim, tiled=True)  174 us
    all_gather x1, waiting for transfers between devices, per_device(): out_full = lax.all_gather(w_out, 'dp', axis=3, tiled=True)  136 us
    all_gather x8, blocking collectives, layer_step(): gathered = lax.all_gather(stream, 'tensor', axis=1, tiled=True)  82.3 us
    all_to_all x8, waiting for transfers between devices, sent_and_summed(): lax.all_to_all(cut_along(value, dim, peers), axis, 0, 0, tiled=True)  67.7 us
    ppermute x8, starting transfers between devices, from_behind(): return lax.ppermute(value, axis, pairs)  61.2 us
    all_to_all x8, starting transfers between devices, sent_and_summed(): lax.all_to_all(cut_along(value, dim, peers), axis, 0, 0, tiled=True)  28.1 us
    dot_general x4, matrix products, attend(): queries = jnp.dot(normed, q_weight, preferred_element_type=jnp.float32)  20.3 us
    dot_general x4, matrix products, layer_step(): jnp.dot(mixed, out_part, preferred_element_type=jnp.float32)  19.8 us
  transfers between devices with their start and end apart: 18, of which 14 were waited for; matrix products, arithmetic and copies ran while one was open for 4% of the time, Pallas kernels for 0%

commit v1 on v0

v1 whole, which is shorter than its diff:
```python
from functools import partial

import jax
import jax.numpy as jnp
from jax import lax
from jax.experimental import pallas as pl
from jax.experimental.pallas import tpu as pltpu
from jax.sharding import PartitionSpec as P

HEAD_DIM = 128
ROPE_THETA = 500000.0
NORM_EPSILON = 1e-05
MESH = pl.DeviceIdType.MESH

LAYERS = 4
NZ, NX, NY = 8, 4, 4
SEQ = 64
WIDTH = 4096
CHUNK = 128
SET = NZ * CHUNK
QKV = 1536
HEADS = 1024
EXTRA = QKV + 128
TOK = NX * SEQ
PIECE = SET // NY


def rope_angles(positions, head_dim):
    half_dim = head_dim // 2
    exponent = jnp.arange(half_dim, dtype=jnp.float32) * (2.0 / head_dim)
    frequency = jnp.float32(ROPE_THETA) ** (-exponent)
    return positions.astype(jnp.float32)[..., None] * frequency


def sample_layout(first_cut, offset, lengths, seq_len):
    places = jnp.arange(seq_len, dtype=jnp.int32)
    positions = jnp.where(places < first_cut, places, places + offset)
    doc_ends = jnp.cumsum(lengths)
    doc_ids = jnp.sum((places[:, None] >= doc_ends[None, :]).astype(jnp.int32), axis=1)
    allowed = (doc_ids[:, None] == doc_ids[None, :]) & (places[None, :] <= places[:, None])
    return (positions, allowed)


def stack_kernel(
    xtok,
    cosines,
    sines,
    bias,
    gain,
    wq,
    wk,
    wv,
    wo,
    out,
    wqkv,
    wob,
    gbuf,
    tsend,
    xbuf,
    xg,
    psend,
    precv,
    abuf,
    osend,
    oown,
    orecv,
    frecv,
    lsem,
    hop_s,
    hop_r,
    own_s,
    own_r,
    par_s,
    par_r,
    g_s,
    g_r,
    t_s,
    t_r,
    x_s,
    x_r,
    p_s,
    p_r,
    a_s,
    a_r,
    o_s,
    o_r,
    f_s,
    f_r,
):
    dp = lax.axis_index("dp")
    p = lax.axis_index("pipe")
    y = lax.axis_index("tensor")
    z = dp // NX
    x = dp % NX
    step = 1 - 2 * p

    def at(zz, xx, pp, yy):
        return {"dp": zz * NX + xx, "pipe": pp, "tensor": yy}

    def zrel(k):
        return (z + step * k + NZ) % NZ

    down = at(zrel(1), x, p, y)
    up = at(zrel(-1), x, p, y)
    other = at(z, x, 1 - p, y)

    def remote(src, dst, s, r, dev):
        return pltpu.make_async_remote_copy(
            src_ref=src, dst_ref=dst, send_sem=s, recv_sem=r, device_id=dev, device_id_type=MESH
        )

    def layer_of(d):
        return p + d * (3 - 2 * p)

    def rows_of(zz):
        return pl.ds(pl.multiple_of(zz * CHUNK, CHUNK), CHUNK)

    def loads(d):
        c = layer_of(d)
        r = rows_of(z)
        return [
            pltpu.make_async_copy(wq.at[d, 0], wqkv.at[c, r, pl.ds(0, 1024)], lsem.at[d, 0]),
            pltpu.make_async_copy(wk.at[d, 0], wqkv.at[c, r, pl.ds(1024, 256)], lsem.at[d, 1]),
            pltpu.make_async_copy(wv.at[d, 0], wqkv.at[c, r, pl.ds(1280, 256)], lsem.at[d, 2]),
            pltpu.make_async_copy(wo.at[d, 0], wob.at[c, :, r], lsem.at[d, 3]),
        ]

    for d in range(2):
        for copy in loads(d):
            copy.start()

    barrier = pltpu.get_barrier_semaphore()
    peers = [down, up, other]
    for i in (1, 2, 3):
        peers.append(at(z, (x + i) % NX, p, y))
        peers.append(at(z, (x + i) % NX, 1 - p, y))
        peers.append(at(z, x, p, (y + i) % NY))
    for dev in peers:
        pl.semaphore_signal(barrier, inc=1, device_id=dev, device_id_type=MESH)
    pl.semaphore_wait(barrier, len(peers))

    def piece(c, zz, t, half):
        if t == 0:
            return wqkv.at[c, pl.ds(pl.multiple_of(zz * CHUNK + half * 64, 64), 64), :]
        return wob.at[c, pl.ds(pl.multiple_of(half * 512, 512), 512), rows_of(zz)]

    def whole(c, zz, t):
        if t == 0:
            return wqkv.at[c, rows_of(zz), :]
        return wob.at[c, :, rows_of(zz)]

    def hop_out(c, t, half, h):
        ref = piece(c, zrel(1 - h), t, half)
        return remote(ref, ref, hop_s.at[c, t, half, h - 1], hop_r.at[c, t, half, h - 1], down)

    def hop_in(c, t, half, h):
        ref = piece(c, zrel(-h), t, half)
        return remote(ref, ref, hop_s.at[c, t, half, h - 1], hop_r.at[c, t, half, h - 1], up)

    def swap_out(c, t, half, h):
        ref = piece(c, zrel(-h), t, half)
        return remote(ref, ref, par_s.at[c, t, half, h - 1], par_r.at[c, t, half, h - 1], other)

    def swap_in(c, t, half, h):
        ref = piece(c, zrel(h), t, half)
        return remote(ref, ref, par_s.at[c, t, half, h - 1], par_r.at[c, t, half, h - 1], other)

    def own_swap(c, t):
        ref = whole(c, z, t)
        return remote(ref, ref, own_s.at[c, t], own_r.at[c, t], other)

    def holder(c):
        return jnp.where((c == 0) | (c == 3), 0, 1)

    def first_hop(c):
        for t in range(2):

            @pl.when(p != holder(c))
            def _():
                own_swap(c, t).wait_recv()

            for half in range(2):
                hop_out(c, t, half, 1).start()

    def forward(c, h):
        for t in range(2):
            for half in range(2):
                hop_in(c, t, half, h).wait_recv()
                if h < 3:
                    hop_out(c, t, half, h + 1).start()
                swap_out(c, t, half, h).start()
            if h == 3:
                hop_out(c, t, p, 4).start()

    def finish(c):
        for t in range(2):
            hop_in(c, t, p, 4).wait_recv()
            swap_out(c, t, p, 4).start()

    def ready(c, t):
        for h in (1, 2, 3):
            for half in range(2):
                swap_in(c, t, half, h).wait_recv()
        swap_in(c, t, 1 - p, 4).wait_recv()

    def load_and_share(d):
        for copy in loads(d):
            copy.wait()
        for t in range(2):
            own_swap(layer_of(d), t).start()

    load_and_share(0)
    first_hop(0)

    for xx in range(NX):
        tsend[xx, :, 0:128] = xtok[:, xx * 128 : xx * 128 + 128]
        tsend[xx, :, 128:256] = xtok[:, 512 + xx * 128 : 512 + xx * 128 + 128]

    def block(ref, b, size):
        return ref.at[pl.ds(pl.multiple_of(b * size, size), size), :]

    def tok_out(i):
        xx = (x + i) % NX
        return remote(
            tsend.at[xx], block(xbuf.at[0, y], x, SEQ), t_s.at[xx], t_r.at[x], at(z, xx, p, y)
        )

    def tok_in(i):
        xx = (x + i) % NX
        return remote(
            tsend.at[xx], block(xbuf.at[0, y], xx, SEQ), t_s.at[xx], t_r.at[xx], at(z, xx, p, y)
        )

    for i in (2, 1, 3):
        tok_out(i).start()
    xbuf[0, y, pl.ds(pl.multiple_of(x * SEQ, SEQ), SEQ), :] = tsend[x]

    load_and_share(1)

    for d in range(2):
        c = layer_of(d)
        for zz in range(NZ):
            row = gain[d, :, pl.ds(pl.multiple_of((zz * NX + x) * CHUNK, CHUNK), CHUNK)]
            gbuf[c, :, zz * CHUNK : zz * CHUNK + CHUNK] = jnp.broadcast_to(row, (8, CHUNK))

    def gain_swap(d, c):
        return remote(gbuf.at[c], gbuf.at[c], g_s.at[d], g_r.at[d], other)

    for d in range(2):
        gain_swap(d, layer_of(d)).start()

    def stream_out(c, i):
        yy = (y + i) % NY
        return remote(xbuf.at[c, y], xbuf.at[c, y], x_s.at[c, yy], x_r.at[c, y], at(z, x, p, yy))

    def stream_in(c, i):
        yy = (y + i) % NY
        return remote(xbuf.at[c, yy], xbuf.at[c, yy], x_s.at[c, yy], x_r.at[c, yy], at(z, x, p, yy))

    for i in (2, 1, 3):
        tok_in(i).wait_recv()
    for i in (2, 1, 3):
        stream_out(0, i).start()

    for h in (1, 2, 3):
        forward(0, h)
    first_hop(1)
    finish(0)
    for d in range(2):
        gain_swap(d, 1 - p + d * (1 + 2 * p)).wait_recv()

    lane = lax.broadcasted_iota(jnp.int32, (SEQ, 128), 1)

    def layer(c, carry):
        for i in (2, 1, 3):
            stream_in(c, i).wait_recv()

        def scale_block(b, carry):
            rows = pl.ds(pl.multiple_of(b * SEQ, SEQ), SEQ)
            total = jnp.zeros((SEQ, 1), jnp.float32)
            for yy in range(NY):
                wide = xbuf[c, yy, rows, :].astype(jnp.float32)
                total = total + jnp.sum(wide * wide, axis=1, keepdims=True)
                row = gbuf[c, 0:1, yy * PIECE : yy * PIECE + PIECE]
                xg[yy, rows, :] = (wide * row).astype(jnp.bfloat16)
            high = total.astype(jnp.bfloat16).astype(jnp.float32)
            mixed = jnp.where(lane == 0, high, jnp.where(lane == 1, total - high, 0.0))
            psend[b, :, QKV:EXTRA] = mixed.astype(jnp.bfloat16)
            return carry

        lax.fori_loop(0, NX, scale_block, 0)
        ready(c, 0)

        def qkv_tile(n, carry):
            cols = pl.ds(pl.multiple_of(n * 256, 256), 256)
            acc = jnp.zeros((TOK, 256), jnp.float32)
            for yy in range(NY):
                acc = acc + jnp.dot(
                    xg[yy],
                    wqkv[c, yy * PIECE : yy * PIECE + PIECE, cols],
                    preferred_element_type=jnp.float32,
                )
            acc = acc.astype(jnp.bfloat16)
            for xx in range(NX):
                psend[xx, :, cols] = acc[xx * SEQ : xx * SEQ + SEQ]
            return carry

        lax.fori_loop(0, QKV // 256, qkv_tile, 0)

        def part_out(i):
            xx = (x + i) % NX
            return remote(psend.at[xx], precv.at[c, x], p_s.at[xx], p_r.at[c, x], at(z, xx, p, y))

        def part_in(i):
            xx = (x + i) % NX
            return remote(psend.at[xx], precv.at[c, xx], p_s.at[xx], p_r.at[c, xx], at(z, xx, p, y))

        for i in (2, 1, 3):
            part_out(i).start()

        @pl.when(c < LAYERS - 1)
        def _():
            forward(c + 1, 1)

        for i in (2, 1, 3):
            part_in(i).wait_recv()
        for i in (2, 1, 3):
            part_out(i).wait_send()

        def summed(b):
            cols = slice(b * 128, b * 128 + 128)
            total = psend[x, :, cols].astype(jnp.float32)
            for i in (1, 2, 3):
                total = total + precv[c, (x + i) % NX, :, cols].astype(jnp.float32)
            return total

        square = jnp.sum(summed(12), axis=1, keepdims=True)
        inv_rms = lax.rsqrt(square * (1.0 / WIDTH) + NORM_EPSILON)
        cos = cosines[...]
        sin = sines[...]

        def turned(b):
            value = summed(b) * inv_rms
            return (value * cos + pltpu.roll(value, 64, 1) * sin).astype(jnp.bfloat16)

        bias4 = jnp.concatenate([bias[...]] * 4, axis=0)
        for g in range(2):
            keys = turned(8 + g)
            vals = (summed(10 + g) * inv_rms).astype(jnp.bfloat16)
            query = jnp.concatenate([turned(g * 4 + j) for j in range(4)], axis=0)
            scores = lax.dot_general(
                query, keys, (((1,), (1,)), ((), ())), preferred_element_type=jnp.float32
            )
            scores = scores * HEAD_DIM ** (-0.5) + bias4
            top = jnp.max(scores, axis=1, keepdims=True)
            expo = jnp.exp(scores - top)
            weights = (expo / jnp.sum(expo, axis=1, keepdims=True)).astype(jnp.bfloat16)
            mixed = jnp.dot(weights, vals, preferred_element_type=jnp.float32).astype(jnp.bfloat16)
            for j in range(4):
                b = g * 4 + j
                abuf[c, x, :, b * 128 : b * 128 + 128] = mixed[j * SEQ : j * SEQ + SEQ]

        def attn_out(i):
            xx = (x + i) % NX
            return remote(abuf.at[c, x], abuf.at[c, x], a_s.at[xx], a_r.at[c, x], at(z, xx, p, y))

        def attn_in(i):
            xx = (x + i) % NX
            return remote(abuf.at[c, xx], abuf.at[c, xx], a_s.at[xx], a_r.at[c, xx], at(z, xx, p, y))

        for i in (2, 1, 3):
            attn_out(i).start()

        @pl.when(c < LAYERS - 1)
        def _():
            forward(c + 1, 2)

        ready(c, 1)
        for i in (2, 1, 3):
            attn_in(i).wait_recv()
        for i in (2, 1, 3):
            attn_out(i).wait_send()

        def proj(yy):
            cols = pl.ds(pl.multiple_of(yy * PIECE, PIECE), PIECE)
            return jnp.dot(
                abuf[c].reshape(TOK, HEADS),
                wob[c, :, cols],
                preferred_element_type=jnp.float32,
            )

        def proj_out(yy):
            return remote(osend.at[yy], orecv.at[c, y], o_s.at[yy], o_r.at[c, y], at(z, x, p, yy))

        def proj_in(yy):
            return remote(osend.at[yy], orecv.at[c, yy], o_s.at[yy], o_r.at[c, yy], at(z, x, p, yy))

        def proj_tile(i, carry):
            yy = (y + i) % NY
            osend[yy] = proj(yy).astype(jnp.bfloat16)
            proj_out(yy).start()
            return carry

        lax.fori_loop(1, NY, proj_tile, 0)
        oown[...] = proj(y)

        @pl.when(c < LAYERS - 1)
        def _():
            forward(c + 1, 3)

        @pl.when(c < LAYERS - 2)
        def _():
            first_hop(c + 2)

        for i in (1, 2, 3):
            proj_in((y + i) % NY).wait_recv()
        for i in (1, 2, 3):
            proj_out((y + i) % NY).wait_send()

        def add_block(b, carry):
            rows = pl.ds(pl.multiple_of(b * SEQ, SEQ), SEQ)
            total = oown[rows, :]
            for i in (1, 2, 3):
                total = total + orecv[c, (y + i) % NY, rows, :].astype(jnp.float32)
            total = total + xbuf[c, y, rows, :].astype(jnp.float32)
            xbuf[c + 1, y, rows, :] = total.astype(jnp.bfloat16)
            return carry

        lax.fori_loop(0, NX, add_block, 0)

        @pl.when(c < LAYERS - 1)
        def _():
            for i in (2, 1, 3):
                stream_out(c + 1, i).start()
            finish(c + 1)

        return carry

    lax.fori_loop(0, LAYERS, layer, 0)

    def done_rows(xx, q):
        return pl.ds(pl.multiple_of(xx * SEQ + q * 32, 32), 32)

    def done_out(i, j):
        xx, q = (x + i) % NX, (p + j) % 2
        return remote(
            xbuf.at[LAYERS, y, done_rows(xx, q), :],
            frecv.at[p, x],
            f_s.at[q, xx],
            f_r.at[p, x],
            at(z, xx, q, y),
        )

    def done_in(i, j):
        xx, q = (x + i) % NX, (p + j) % 2
        return remote(
            xbuf.at[LAYERS, y, done_rows(xx, q), :],
            frecv.at[q, xx],
            f_s.at[q, xx],
            f_r.at[q, xx],
            at(z, xx, q, y),
        )

    away = [(i, j) for i in (2, 1, 3, 0) for j in range(2) if (i, j) != (0, 0)]
    for i, j in away:
        done_out(i, j).start()
    frecv[p, x] = xbuf[LAYERS, y, done_rows(x, p), :]
    for i, j in away:
        done_in(i, j).wait_recv()
    for q in range(2):
        for xx in range(NX):
            out[q, :, xx * 128 : xx * 128 + 128] = frecv[q, xx, :, 0:128]
            out[q, :, 512 + xx * 128 : 512 + xx * 128 + 128] = frecv[q, xx, :, 128:256]

    for i, j in away:
        done_out(i, j).wait_send()
    for i in (1, 2, 3):
        tok_out(i).wait_send()
    for d in range(2):
        gain_swap(d, layer_of(d)).wait_send()
        for t in range(2):
            own_swap(layer_of(d), t).wait_send()

    def drain(c, carry):
        for t in range(2):
            for half in range(2):
                for h in (1, 2, 3):
                    hop_out(c, t, half, h).wait_send()
                    swap_out(c, t, half, h).wait_send()
            hop_out(c, t, p, 4).wait_send()
            swap_out(c, t, p, 4).wait_send()

        @pl.when(c < LAYERS - 1)
        def _():
            for i in (1, 2, 3):
                stream_out(c, i).wait_send()

        @pl.when(c == LAYERS - 1)
        def _():
            for i in (1, 2, 3):
                stream_out(c, i).wait_send()

        return carry

    lax.fori_loop(0, LAYERS, drain, 0)


def per_device(
    tokens,
    w_query,
    w_key,
    w_value,
    w_out,
    norm_gain,
    boundary,
    skip_offset,
    doc_lengths,
    batch_order,
):
    core = lax.axis_index("pipe")
    sample = lax.dynamic_index_in_dim(batch_order[0], core, 0, keepdims=False)

    def chosen(array):
        return lax.dynamic_index_in_dim(array, sample, 0, keepdims=False)

    positions, allowed = sample_layout(
        chosen(boundary), chosen(skip_offset), chosen(doc_lengths), SEQ
    )
    angles = rope_angles(positions, HEAD_DIM)
    cosine = jnp.cos(angles)
    sine = jnp.sin(angles)
    cosines = jnp.concatenate([cosine, cosine], axis=1)
    sines = jnp.concatenate([-sine, sine], axis=1)
    bias = jnp.where(allowed, 0.0, -jnp.inf).astype(jnp.float32)

    vmem = pl.BlockSpec(memory_space=pltpu.VMEM)
    anywhere = pl.BlockSpec(memory_space=pl.ANY)
    dma = pltpu.SemaphoreType.DMA
    bf16, f32 = jnp.bfloat16, jnp.float32
    return pl.pallas_call(
        stack_kernel,
        out_shape=jax.ShapeDtypeStruct((2, 32, 1024), bf16),
        in_specs=[vmem] * 5 + [anywhere] * 4,
        out_specs=vmem,
        scratch_shapes=[
            pltpu.VMEM((LAYERS, SET, QKV), bf16),
            pltpu.VMEM((LAYERS, HEADS, SET), bf16),
            pltpu.VMEM((LAYERS, 8, SET), f32),
            pltpu.VMEM((NX, SEQ, PIECE), bf16),
            pltpu.VMEM((LAYERS + 1, NY, TOK, PIECE), bf16),
            pltpu.VMEM((NY, TOK, PIECE), bf16),
            pltpu.VMEM((NX, SEQ, EXTRA), bf16),
            pltpu.VMEM((LAYERS, NX, SEQ, EXTRA), bf16),
            pltpu.VMEM((LAYERS, NX, SEQ, HEADS), bf16),
            pltpu.VMEM((NY, TOK, PIECE), bf16),
            pltpu.VMEM((TOK, PIECE), f32),
            pltpu.VMEM((LAYERS, NY, TOK, PIECE), bf16),
            pltpu.VMEM((2, NX, 32, PIECE), bf16),
            dma((2, 4)),
            dma((LAYERS, 2, 2, 4)),
            dma((LAYERS, 2, 2, 4)),
            dma((LAYERS, 2)),
            dma((LAYERS, 2)),
            dma((LAYERS, 2, 2, 4)),
            dma((LAYERS, 2, 2, 4)),
            dma((2,)),
            dma((2,)),
            dma((NX,)),
            dma((NX,)),
            dma((LAYERS, NY)),
            dma((LAYERS, NY)),
            dma((NX,)),
            dma((LAYERS, NX)),
            dma((NX,)),
            dma((LAYERS, NX)),
            dma((NY,)),
            dma((LAYERS, NY)),
            dma((2, NX)),
            dma((2, NX)),
        ],
        compiler_params=pltpu.CompilerParams(
            collective_id=0, has_side_effects=True, vmem_limit_bytes=60 * 1024 * 1024
        ),
    )(chosen(tokens), cosines, sines, bias, norm_gain, w_query, w_key, w_value, w_out)


def solution(mesh):
    placed = (
        P("dp", None, "tensor"),
        P(None, "pipe", "dp", "tensor"),
        P(None, "pipe", "dp", "tensor"),
        P(None, "pipe", "dp", "tensor"),
        P(None, "pipe", "tensor", "dp"),
        P(None, "pipe", None),
        P("dp"),
        P("dp"),
        P("dp", None),
        P("dp", None),
    )
    return jax.shard_map(
        per_device, mesh=mesh, in_specs=placed, out_specs=P("dp", "pipe", "tensor"), check_vma=False
    )
```

time: 727 us -> 197 us (0.27)
  waiting for transfers between devices: 383 us -> 0 us
  Pallas kernels: 0 us -> 186 us
  starting transfers between devices: 89.4 us -> 0 us
  blocking collectives: 84.6 us -> 0 us
  matrix products: 60.5 us -> 0 us
  local copies, waits for them, and re-layouts: 62.1 us -> 5.39 us
  other arithmetic: 24 us -> 3.16 us
  between operations: 13.5 us -> 2.02 us
  loops' own time: 8.27 us -> 0 us
    all_gather x2 -> x0, waiting for transfers between devices: 310 us -> none  [the longest x1 174 us: sent_together(): whole = lax.all_gather(both, axis, axis=dim, tiled=True)]
    pallas_call x0 -> x1, Pallas kernels: none -> 186 us  [per_device(): pl.pallas_call(stack_kernel, out_shape=jax.ShapeDtypeStruct((2, 32, 1024)...]
    all_gather x9 -> x0, blocking collectives: 84.6 us -> none  [the longest x8 82.3 us: layer_step(): gathered = lax.all_gather(stream, 'tensor', axis=1, tiled=True)]
    all_to_all x8 -> x0, waiting for transfers between devices: 67.7 us -> none  [sent_and_summed(): lax.all_to_all(cut_along(value, dim, peers), axis, 0, 0, tiled=True)]
    ppermute x8 -> x0, starting transfers between devices: 61.2 us -> none  [from_behind(): return lax.ppermute(value, axis, pairs)]
    dot_general x20 -> x0, matrix products: 59 us -> none  [the longest x4 20.3 us: attend(): queries = jnp.dot(normed, q_weight, preferred_element_type=jnp.float32)]
    squeeze x7 -> x1, local copies, waits for them, and re-layouts: 29.7 us -> 0.66 us  [chosen(): return lax.dynamic_index_in_dim(array, sample, 0, keepdims=False)]
    all_to_all x8 -> x0, starting transfers between devices: 28.1 us -> none  [sent_and_summed(): lax.all_to_all(cut_along(value, dim, peers), axis, 0, 0, tiled=True)]
  transfers between devices with their start and end apart: 18 -> 0, of which waited for: 14 -> 0; matrix products, arithmetic and copies ran while one was open for 4% -> 0% of each run, Pallas kernels for 0% -> 0%
where the time goes in v1:
time: 197 us
  Pallas kernels  186 us (94%)
  local copies, waits for them, and re-layouts  5.39 us (3%)
  other arithmetic  3.16 us (2%)
  between operations  2.02 us (1%)
    pallas_call x1, Pallas kernels, per_device(): pl.pallas_call(stack_kernel, out_shape=jax.ShapeDtypeStruct((2, 32, 1024)...  186 us

profile of v1, /device:TPU:1, one launch (start us, length us, event | category | flops | bytes accessed | tf_op | source)
XLA Modules:
  0.0 196.6 jit_solution(1833682917516977075)
XLA Ops:
  0.0 0.0 copy-start
  0.0 0.0 copy-start.2
  0.0 0.7 copy-done.2
  0.7 0.6 constant_dynamic-slice_fusion.1
  2.6 0.0 copy-start.3
  3.3 0.0 copy-done.3
  3.3 0.6 dynamic_slice.21
  3.9 0.0 copy-start.4
  3.9 0.7 copy-done.4
  4.5 0.6 dynamic_slice.20
  5.1 0.0 copy-start.1
  5.1 1.3 fusion.4
  6.4 0.0 copy-done.1
  6.4 0.2 reduce-window.8
  6.6 0.1 convert_reduce_fusion
  6.7 0.7 fusion.1.bias
  7.4 0.2 fusion.2
  7.6 0.7 pad_maximum_fusion
  8.3 0.0 copy-done
  8.3 0.7 dynamic-slice_bitcast_fusion.xtok
  9.0 186.1 %shard_map.100 = bf16[2,32,1024]{2,1,0:T(8,128)(2,1)} custom-call(bf16[64,1024]{1,0:T(8,128)(2,1)} %dynamic-slice_bitcast_fusion.xtok, f32[64,128]{1,0:T(8,128)} %get-tuple-element.8.cosines, f32[64,128]{1,0:T(8,128)} %get-tuple-element.9.sines, f32[64,64]{1,0:T(8,128)} %fusion.1.bias, f32[2,1,4096]{2,1,0:T(1,128)} %gain.1, bf16[2,1,128,1024]{3,2,1,0:T(8,128)(2,1)} %wq.1, ...), custom_call_target="tpu_custom_call" | custom-call | tf_op jit(solution)/shard_map/pallas_call | solution.py:540
  195.1 1.6 copy.12
  (2 shorter events, 0.0 us)
Async XLA Ops:
  0.0 8.3 %copy-start = (bf16[2,64,1024]{2,1,0:T(8,128)(2,1)S(1)}, bf16[2,64,1024]{2,1,0:T(8,128)(2,1)}, u32[]{:S(2)}) copy-start(bf16[2,64,1024]{2,1,0:T(8,128)(2,1)} %param.10) | copy-start | bytes 786436
  0.0 0.7 copy-start.2
  2.6 0.7 copy-start.3
  3.9 0.7 copy-start.4
  5.1 1.3 copy-start.1

commit v2 on v1

--- a/solution.py
+++ b/solution.py
@@ -1,7 +1,8 @@
-from functools import partial
+import math
 
 import jax
 import jax.numpy as jnp
+import numpy as np
 from jax import lax
 from jax.experimental import pallas as pl
 from jax.experimental.pallas import tpu as pltpu
@@ -20,33 +21,48 @@
 SET = NZ * CHUNK
 QKV = 1536
 HEADS = 1024
-EXTRA = QKV + 128
+GROUP = QKV // 2
+EXTRA = GROUP + 128
+HALF = HEADS // 2
 TOK = NX * SEQ
 PIECE = SET // NY
 
 
-def rope_angles(positions, head_dim):
-    half_dim = head_dim // 2
-    exponent = jnp.arange(half_dim, dtype=jnp.float32) * (2.0 / head_dim)
-    frequency = jnp.float32(ROPE_THETA) ** (-exponent)
-    return positions.astype(jnp.float32)[..., None] * frequency
-
-
-def sample_layout(first_cut, offset, lengths, seq_len):
-    places = jnp.arange(seq_len, dtype=jnp.int32)
-    positions = jnp.where(places < first_cut, places, places + offset)
-    doc_ends = jnp.cumsum(lengths)
-    doc_ids = jnp.sum((places[:, None] >= doc_ends[None, :]).astype(jnp.int32), axis=1)
-    allowed = (doc_ids[:, None] == doc_ids[None, :]) & (places[None, :] <= places[:, None])
-    return (positions, allowed)
+TWO_PI_HIGH = 6.28125
+TWO_PI_MID = 0.0019340515136718750
+TWO_PI_LOW = 2 * math.pi - TWO_PI_HIGH - TWO_PI_MID
+SINE_TERMS = [(-1.0) ** k / math.factorial(2 * k + 1) for k in range(10)]
+COSINE_TERMS = [(-1.0) ** k / math.factorial(2 * k) for k in range(11)]
+
+
+def frequencies():
+    half = HEAD_DIM // 2
+    table = np.float64(ROPE_THETA) ** (-np.arange(half, dtype=np.float64) / half)
+    return np.tile(table.astype(np.float32), 2)[None, :].repeat(8, axis=0)
+
+
+def series(terms, square):
+    total = jnp.full(square.shape, terms[-1], jnp.float32)
+    for term in terms[-2::-1]:
+        total = total * square + term
+    return total
+
+
+def sine_and_cosine(angle):
+    turns = jnp.floor(angle * (0.5 / math.pi) + 0.5)
+    rest = ((angle - turns * TWO_PI_HIGH) - turns * TWO_PI_MID) - turns * TWO_PI_LOW
+    square = rest * rest
+    return rest * series(SINE_TERMS, square), series(COSINE_TERMS, square)
 
 
 def stack_kernel(
-    xtok,
-    cosines,
-    sines,
-    bias,
-    gain,
+    order,
+    boundary,
+    offset,
+    lengths,
+    tokens,
+    freq,
+    gain_in,
     wq,
     wk,
     wv,
@@ -58,13 +74,22 @@
     tsend,
     xbuf,
     xg,
-    psend,
-    precv,
+    psend0,
+    psend1,
+    precv0,
+    precv1,
     abuf,
     osend,
     oown,
     orecv,
     frecv,
+    tok_v,
+    freq_v,
+    gain,
+    cosines,
+    sines,
+    bias,
+    isem,
     lsem,
     hop_s,
     hop_r,
@@ -118,16 +143,27 @@
     def loads(d):
         c = layer_of(d)
         r = rows_of(z)
-        return [
-            pltpu.make_async_copy(wq.at[d, 0], wqkv.at[c, r, pl.ds(0, 1024)], lsem.at[d, 0]),
-            pltpu.make_async_copy(wk.at[d, 0], wqkv.at[c, r, pl.ds(1024, 256)], lsem.at[d, 1]),
-            pltpu.make_async_copy(wv.at[d, 0], wqkv.at[c, r, pl.ds(1280, 256)], lsem.at[d, 2]),
-            pltpu.make_async_copy(wo.at[d, 0], wob.at[c, :, r], lsem.at[d, 3]),
-        ]
-
-    for d in range(2):
-        for copy in loads(d):
-            copy.start()
+        copies = []
+        for g in range(2):
+            for k, (source, width, first) in enumerate(
+                ((wq, 512, 0), (wk, 128, 512), (wv, 128, 640))
+            ):
+                copies.append(
+                    pltpu.make_async_copy(
+                        source.at[d, 0, :, pl.ds(g * width, width)],
+                        wqkv.at[c, r, pl.ds(g * GROUP + first, width)],
+                        lsem.at[d, g * 3 + k],
+                    )
+                )
+        return copies, [pltpu.make_async_copy(wo.at[d, 0], wob.at[c, :, r], lsem.at[d, 6])]
+
+    small = [
+        pltpu.make_async_copy(tokens, tok_v, isem.at[0]),
+        pltpu.make_async_copy(freq, freq_v, isem.at[1]),
+        pltpu.make_async_copy(gain_in, gain, isem.at[2]),
+    ]
+    for copy in loads(0)[0] + loads(0)[1] + small + loads(1)[0] + loads(1)[1]:
+        copy.start()
 
     barrier = pltpu.get_barrier_semaphore()
     peers = [down, up, other]
@@ -172,30 +208,26 @@
     def holder(c):
         return jnp.where((c == 0) | (c == 3), 0, 1)
 
-    def first_hop(c):
-        for t in range(2):
-
-            @pl.when(p != holder(c))
-            def _():
-                own_swap(c, t).wait_recv()
-
-            for half in range(2):
-                hop_out(c, t, half, 1).start()
-
-    def forward(c, h):
-        for t in range(2):
-            for half in range(2):
-                hop_in(c, t, half, h).wait_recv()
-                if h < 3:
-                    hop_out(c, t, half, h + 1).start()
-                swap_out(c, t, half, h).start()
-            if h == 3:
-                hop_out(c, t, p, 4).start()
-
-    def finish(c):
-        for t in range(2):
-            hop_in(c, t, p, 4).wait_recv()
-            swap_out(c, t, p, 4).start()
+    def first_hop(c, t):
+        @pl.when(p != holder(c))
+        def _():
+            own_swap(c, t).wait_recv()
+
+        for half in range(2):
+            hop_out(c, t, half, 1).start()
+
+    def forward(c, t, h):
+        for half in range(2):
+            hop_in(c, t, half, h).wait_recv()
+            if h < 3:
+                hop_out(c, t, half, h + 1).start()
+            swap_out(c, t, half, h).start()
+        if h == 3:
+            hop_out(c, t, p, 4).start()
+
+    def finish(c, t):
+        hop_in(c, t, p, 4).wait_recv()
+        swap_out(c, t, p, 4).start()
 
     def ready(c, t):
         for h in (1, 2, 3):
@@ -204,17 +236,27 @@
         swap_in(c, t, 1 - p, 4).wait_recv()
 
     def load_and_share(d):
-        for copy in loads(d):
-            copy.wait()
         for t in range(2):
+            for copy in loads(d)[t]:
+                copy.wait()
             own_swap(layer_of(d), t).start()
 
     load_and_share(0)
-    first_hop(0)
+    first_hop(0, 0)
+
+    for copy in small:
+        copy.wait()
+    second = order[0, p] == 1
+
+    def chosen(first, other_one):
+        return jnp.where(second, other_one, first)
 
     for xx in range(NX):
-        tsend[xx, :, 0:128] = xtok[:, xx * 128 : xx * 128 + 128]
-        tsend[xx, :, 128:256] = xtok[:, 512 + xx * 128 : 512 + xx * 128 + 128]
+        for k in range(2):
+            cols = slice(k * 512 + xx * 128, k * 512 + xx * 128 + 128)
+            tsend[xx, :, k * 128 : k * 128 + 128] = chosen(
+                tok_v[0, :, cols].astype(jnp.float32), tok_v[1, :, cols].astype(jnp.float32)
+            ).astype(jnp.bfloat16)
 
     def block(ref, b, size):
         return ref.at[pl.ds(pl.multiple_of(b * size, size), size), :]
@@ -235,6 +277,7 @@
         tok_out(i).start()
     xbuf[0, y, pl.ds(pl.multiple_of(x * SEQ, SEQ), SEQ), :] = tsend[x]
 
+    forward(0, 0, 1)
     load_and_share(1)
 
     for d in range(2):
@@ -262,17 +305,54 @@
     for i in (2, 1, 3):
         stream_out(0, i).start()
 
-    for h in (1, 2, 3):
-        forward(0, h)
-    first_hop(1)
-    finish(0)
+    forward(0, 0, 2)
+
+    row = lax.broadcasted_iota(jnp.int32, (SEQ, 128), 0)
+    lane = lax.broadcasted_iota(jnp.int32, (SEQ, 128), 1)
+    cut = chosen(boundary[0], boundary[1])
+    jump = chosen(offset[0], offset[1])
+    places = jnp.where(row < cut, row, row + jump)
+    sine, cosine = sine_and_cosine(places.astype(jnp.float32) * freq_v[0:1, :])
+    cosines[...] = cosine
+    sines[...] = jnp.where(lane < 64, -sine, sine)
+    from_row = lax.broadcasted_iota(jnp.int32, (SEQ, SEQ), 0)
+    to_row = lax.broadcasted_iota(jnp.int32, (SEQ, SEQ), 1)
+    end = 0
+    doc_from = jnp.zeros((SEQ, SEQ), jnp.int32)
+    doc_to = jnp.zeros((SEQ, SEQ), jnp.int32)
+    for k in range(4):
+        end = end + chosen(lengths[0, k], lengths[1, k])
+        doc_from = doc_from + jnp.where(from_row >= end, 1, 0)
+        doc_to = doc_to + jnp.where(to_row >= end, 1, 0)
+    allowed = (doc_from == doc_to) & (to_row <= from_row)
+    mask = jnp.where(allowed, 0.0, -jnp.inf).astype(jnp.float32)
+    for j in range(4):
+        bias[j * SEQ : j * SEQ + SEQ, :] = mask
+
+    forward(0, 0, 3)
+    first_hop(0, 1)
     for d in range(2):
         gain_swap(d, 1 - p + d * (1 + 2 * p)).wait_recv()
 
-    lane = lax.broadcasted_iota(jnp.int32, (SEQ, 128), 1)
-
     def layer(c, carry):
-        for i in (2, 1, 3):
+        last = c == LAYERS - 1
+
+        @pl.when(c > 0)
+        def _():
+            forward(c, 1, 1)
+
+        finish(c, 0)
+        stream_in(c, 1).wait_recv()
+
+        @pl.when(c > 0)
+        def _():
+            forward(c, 1, 2)
+
+            @pl.when(jnp.logical_not(last))
+            def _():
+                first_hop(c + 1, 0)
+
+        for i in (3, 2):
             stream_in(c, i).wait_recv()
 
         def scale_block(b, carry):
@@ -285,14 +365,14 @@
                 xg[yy, rows, :] = (wide * row).astype(jnp.bfloat16)
             high = total.astype(jnp.bfloat16).astype(jnp.float32)
             mixed = jnp.where(lane == 0, high, jnp.where(lane == 1, total - high, 0.0))
-            psend[b, :, QKV:EXTRA] = mixed.astype(jnp.bfloat16)
+            psend0[b, :, GROUP:EXTRA] = mixed.astype(jnp.bfloat16)
             return carry
 
         lax.fori_loop(0, NX, scale_block, 0)
         ready(c, 0)
 
-        def qkv_tile(n, carry):
-            cols = pl.ds(pl.multiple_of(n * 256, 256), 256)
+        def qkv_tile(n, g, psend):
+            cols = pl.ds(pl.multiple_of(g * GROUP + n * 256, 256), 256)
             acc = jnp.zeros((TOK, 256), jnp.float32)
             for yy in range(NY):
                 acc = acc + jnp.dot(
@@ -302,92 +382,116 @@
                 )
             acc = acc.astype(jnp.bfloat16)
             for xx in range(NX):
-                psend[xx, :, cols] = acc[xx * SEQ : xx * SEQ + SEQ]
-            return carry
-
-        lax.fori_loop(0, QKV // 256, qkv_tile, 0)
-
-        def part_out(i):
+                psend[xx, :, pl.ds(pl.multiple_of(n * 256, 256), 256)] = acc[
+                    xx * SEQ : xx * SEQ + SEQ
+                ]
+            return 0
+
+        sends = (psend0, psend1)
+        lands = (precv0, precv1)
+
+        def part_out(g, i):
             xx = (x + i) % NX
-            return remote(psend.at[xx], precv.at[c, x], p_s.at[xx], p_r.at[c, x], at(z, xx, p, y))
-
-        def part_in(i):
+            return remote(
+                sends[g].at[xx], lands[g].at[c, x], p_s.at[g, xx], p_r.at[g, c, x], at(z, xx, p, y)
+            )
+
+        def part_in(g, i):
             xx = (x + i) % NX
-            return remote(psend.at[xx], precv.at[c, xx], p_s.at[xx], p_r.at[c, xx], at(z, xx, p, y))
-
-        for i in (2, 1, 3):
-            part_out(i).start()
-
-        @pl.when(c < LAYERS - 1)
-        def _():
-            forward(c + 1, 1)
-
-        for i in (2, 1, 3):
-            part_in(i).wait_recv()
-        for i in (2, 1, 3):
-            part_out(i).wait_send()
-
-        def summed(b):
+            return remote(
+                sends[g].at[xx], lands[g].at[c, xx], p_s.at[g, xx], p_r.at[g, c, xx], at(z, xx, p, y)
+            )
+
+        def attn_out(g, i):
+            xx = (x + i) % NX
+            ref = abuf.at[c, g, x]
+            return remote(ref, ref, a_s.at[g, xx], a_r.at[g, c, x], at(z, xx, p, y))
+
+        def attn_in(g, i):
+            xx = (x + i) % NX
+            ref = abuf.at[c, g, xx]
+            return remote(ref, ref, a_s.at[g, xx], a_r.at[g, c, xx], at(z, xx, p, y))
+
+        for g in range(2):
+            lax.fori_loop(0, GROUP // 256, lambda n, _: qkv_tile(n, g, sends[g]), 0)
+            for i in (2, 1, 3):
+                part_out(g, i).start()
+
+        @pl.when(c == 0)
+        def _():
+            forward(c, 1, 1)
+            first_hop(c + 1, 0)
+            forward(c, 1, 2)
+
+        def summed(g, b):
             cols = slice(b * 128, b * 128 + 128)
-            total = psend[x, :, cols].astype(jnp.float32)
+            total = sends[g][x, :, cols].astype(jnp.float32)
             for i in (1, 2, 3):
-                total = total + precv[c, (x + i) % NX, :, cols].astype(jnp.float32)
+                total = total + lands[g][c, (x + i) % NX, :, cols].astype(jnp.float32)
             return total
 
-        square = jnp.sum(summed(12), axis=1, keepdims=True)
-        inv_rms = lax.rsqrt(square * (1.0 / WIDTH) + NORM_EPSILON)
-        cos = cosines[...]
-        sin = sines[...]
-
-        def turned(b):
-            value = summed(b) * inv_rms
-            return (value * cos + pltpu.roll(value, 64, 1) * sin).astype(jnp.bfloat16)
-
-        bias4 = jnp.concatenate([bias[...]] * 4, axis=0)
+        inv_rms = None
         for g in range(2):
-            keys = turned(8 + g)
-            vals = (summed(10 + g) * inv_rms).astype(jnp.bfloat16)
-            query = jnp.concatenate([turned(g * 4 + j) for j in range(4)], axis=0)
+            for i in (1, 3, 2):
+                part_in(g, i).wait_recv()
+            if g == 0:
+                square = jnp.sum(summed(0, 6), axis=1, keepdims=True)
+                inv_rms = lax.rsqrt(square * (1.0 / WIDTH) + NORM_EPSILON)
+
+            def turned(b):
+                value = summed(g, b) * inv_rms
+                return (value * cosines[...] + pltpu.roll(value, 64, 1) * sines[...]).astype(
+                    jnp.bfloat16
+                )
+
+            keys = turned(4)
+            vals = (summed(g, 5) * inv_rms).astype(jnp.bfloat16)
+            query = jnp.concatenate([turned(j) for j in range(4)], axis=0)
             scores = lax.dot_general(
                 query, keys, (((1,), (1,)), ((), ())), preferred_element_type=jnp.float32
             )
-            scores = scores * HEAD_DIM ** (-0.5) + bias4
+            scores = scores * HEAD_DIM ** (-0.5) + bias[...]
             top = jnp.max(scores, axis=1, keepdims=True)
             expo = jnp.exp(scores - top)
             weights = (expo / jnp.sum(expo, axis=1, keepdims=True)).astype(jnp.bfloat16)
             mixed = jnp.dot(weights, vals, preferred_element_type=jnp.float32).astype(jnp.bfloat16)
             for j in range(4):
-                b = g * 4 + j
-                abuf[c, x, :, b * 128 : b * 128 + 128] = mixed[j * SEQ : j * SEQ + SEQ]
-
-        def attn_out(i):
-            xx = (x + i) % NX
-            return remote(abuf.at[c, x], abuf.at[c, x], a_s.at[xx], a_r.at[c, x], at(z, xx, p, y))
-
-        def attn_in(i):
-            xx = (x + i) % NX
-            return remote(abuf.at[c, xx], abuf.at[c, xx], a_s.at[xx], a_r.at[c, xx], at(z, xx, p, y))
-
-        for i in (2, 1, 3):
-            attn_out(i).start()
-
-        @pl.when(c < LAYERS - 1)
-        def _():
-            forward(c + 1, 2)
+                abuf[c, g, x, :, j * 128 : j * 128 + 128] = mixed[j * SEQ : j * SEQ + SEQ]
+            for i in (2, 1, 3):
+                attn_out(g, i).start()
+            if g == 0:
+                forward(c, 1, 3)
+
+                @pl.when(jnp.logical_not(last))
+                def _():
+                    forward(c + 1, 0, 1)
+
+        finish(c, 1)
+        for i in (1, 3, 2):
+            attn_in(0, i).wait_recv()
+
+        @pl.when(jnp.logical_not(last))
+        def _():
+            forward(c + 1, 0, 2)
 
         ready(c, 1)
-        for i in (2, 1, 3):
-            attn_in(i).wait_recv()
-        for i in (2, 1, 3):
-            attn_out(i).wait_send()
+        for i in (1, 3, 2):
+            attn_in(1, i).wait_recv()
+        for g in range(2):
+            for i in (1, 2, 3):
+                part_out(g, i).wait_send()
+                attn_out(g, i).wait_send()
 
         def proj(yy):
             cols = pl.ds(pl.multiple_of(yy * PIECE, PIECE), PIECE)
-            return jnp.dot(
-                abuf[c].reshape(TOK, HEADS),
-                wob[c, :, cols],
-                preferred_element_type=jnp.float32,
-            )
+            total = jnp.zeros((TOK, PIECE), jnp.float32)
+            for g in range(2):
+                total = total + jnp.dot(
+                    abuf[c, g].reshape(TOK, HALF),
+                    wob[c, g * HALF : g * HALF + HALF, cols],
+                    preferred_element_type=jnp.float32,
+                )
+            return total
 
         def proj_out(yy):
             return remote(osend.at[yy], orecv.at[c, y], o_s.at[yy], o_r.at[c, y], at(z, x, p, yy))
@@ -404,15 +508,17 @@
         lax.fori_loop(1, NY, proj_tile, 0)
         oown[...] = proj(y)
 
-        @pl.when(c < LAYERS - 1)
-        def _():
-            forward(c + 1, 3)
-
-        @pl.when(c < LAYERS - 2)
-        def _():
-            first_hop(c + 2)
-
-        for i in (1, 2, 3):
+        @pl.when(jnp.logical_not(last))
+        def _():
+            first_hop(c + 1, 1)
+
+        proj_in((y + 1) % NY).wait_recv()
+
+        @pl.when(jnp.logical_not(last))
+        def _():
+            forward(c + 1, 0, 3)
+
+        for i in (3, 2):
             proj_in((y + i) % NY).wait_recv()
         for i in (1, 2, 3):
             proj_out((y + i) % NY).wait_send()
@@ -432,7 +538,6 @@
         def _():
             for i in (2, 1, 3):
                 stream_out(c + 1, i).start()
-            finish(c + 1)
 
         return carry
 
@@ -517,30 +622,15 @@
     doc_lengths,
     batch_order,
 ):
-    core = lax.axis_index("pipe")
-    sample = lax.dynamic_index_in_dim(batch_order[0], core, 0, keepdims=False)
-
-    def chosen(array):
-        return lax.dynamic_index_in_dim(array, sample, 0, keepdims=False)
-
-    positions, allowed = sample_layout(
-        chosen(boundary), chosen(skip_offset), chosen(doc_lengths), SEQ
-    )
-    angles = rope_angles(positions, HEAD_DIM)
-    cosine = jnp.cos(angles)
-    sine = jnp.sin(angles)
-    cosines = jnp.concatenate([cosine, cosine], axis=1)
-    sines = jnp.concatenate([-sine, sine], axis=1)
-    bias = jnp.where(allowed, 0.0, -jnp.inf).astype(jnp.float32)
-
     vmem = pl.BlockSpec(memory_space=pltpu.VMEM)
+    smem = pl.BlockSpec(memory_space=pltpu.SMEM)
     anywhere = pl.BlockSpec(memory_space=pl.ANY)
     dma = pltpu.SemaphoreType.DMA
     bf16, f32 = jnp.bfloat16, jnp.float32
     return pl.pallas_call(
         stack_kernel,
         out_shape=jax.ShapeDtypeStruct((2, 32, 1024), bf16),
-        in_specs=[vmem] * 5 + [anywhere] * 4,
+        in_specs=[smem] * 4 + [anywhere] * 7,
         out_specs=vmem,
         scratch_shapes=[
             pltpu.VMEM((LAYERS, SET, QKV), bf16),
@@ -550,13 +640,22 @@
             pltpu.VMEM((LAYERS + 1, NY, TOK, PIECE), bf16),
             pltpu.VMEM((NY, TOK, PIECE), bf16),
             pltpu.VMEM((NX, SEQ, EXTRA), bf16),
+            pltpu.VMEM((NX, SEQ, GROUP), bf16),
             pltpu.VMEM((LAYERS, NX, SEQ, EXTRA), bf16),
-            pltpu.VMEM((LAYERS, NX, SEQ, HEADS), bf16),
+            pltpu.VMEM((LAYERS, NX, SEQ, GROUP), bf16),
+            pltpu.VMEM((LAYERS, 2, NX, SEQ, HALF), bf16),
             pltpu.VMEM((NY, TOK, PIECE), bf16),
             pltpu.VMEM((TOK, PIECE), f32),
             pltpu.VMEM((LAYERS, NY, TOK, PIECE), bf16),
             pltpu.VMEM((2, NX, 32, PIECE), bf16),
-            dma((2, 4)),
+            pltpu.VMEM((2, SEQ, 1024), bf16),
+            pltpu.VMEM((8, HEAD_DIM), f32),
+            pltpu.VMEM((2, 1, WIDTH), f32),
+            pltpu.VMEM((SEQ, HEAD_DIM), f32),
+            pltpu.VMEM((SEQ, HEAD_DIM), f32),
+            pltpu.VMEM((4 * SEQ, SEQ), f32),
+            dma((3,)),
+            dma((2, 7)),
             dma((LAYERS, 2, 2, 4)),
             dma((LAYERS, 2, 2, 4)),
             dma((LAYERS, 2)),
@@ -569,10 +668,10 @@
             dma((NX,)),
             dma((LAYERS, NY)),
             dma((LAYERS, NY)),
-            dma((NX,)),
-            dma((LAYERS, NX)),
-            dma((NX,)),
-            dma((LAYERS, NX)),
+            dma((2, NX)),
+            dma((2, LAYERS, NX)),
+            dma((2, NX)),
+            dma((2, LAYERS, NX)),
             dma((NY,)),
             dma((LAYERS, NY)),
             dma((2, NX)),
@@ -581,7 +680,19 @@
         compiler_params=pltpu.CompilerParams(
             collective_id=0, has_side_effects=True, vmem_limit_bytes=60 * 1024 * 1024
         ),
-    )(chosen(tokens), cosines, sines, bias, norm_gain, w_query, w_key, w_value, w_out)
+    )(
+        batch_order,
+        boundary,
+        skip_offset,
+        doc_lengths,
+        tokens,
+        jnp.asarray(frequencies()),
+        norm_gain,
+        w_query,
+        w_key,
+        w_value,
+        w_out,
+    )
 
 
 def solution(mesh):

time: 197 us -> 175 us (0.89)
  Pallas kernels: 186 us -> 173 us
  local copies, waits for them, and re-layouts: 5.39 us -> 1.57 us
  other arithmetic: 3.16 us -> 0 us
  between operations: 2.02 us -> 0.01 us
    pallas_call x1, Pallas kernels: 186 us -> 173 us  [per_device(): pl.pallas_call(stack_kernel, out_shape=jax.ShapeDtypeStruct((2, 32, 1024)...]
where the time goes in v2:
time: 175 us
  Pallas kernels  173 us (99%)
    pallas_call x1, Pallas kernels, per_device(): pl.pallas_call(stack_kernel, out_shape=jax.ShapeDtypeStruct((2, 32, 1024)...  173 us

profile of v2, /device:TPU:1, one launch (start us, length us, event | category | flops | bytes accessed | tf_op | source)
XLA Modules:
  0.0 174.9 jit_solution(4527126093074354831)
XLA Ops:
  0.0 173.3 %shard_map.109 = bf16[2,32,1024]{2,1,0:T(8,128)(2,1)} custom-call(s32[1,2]{1,0:T(1,128)} %order.1, s32[2]{0:T(128)} %boundary.1, s32[2]{0:T(128)} %offset.1, s32[2,4]{1,0:T(2,128)} %lengths.1, bf16[2,64,1024]{2,1,0:T(8,128)(2,1)} %tokens.1, f32[8,128]{1,0:T(8,128)} %constant.2.clone.freq, f32[2,1,4096]{2,1,0:T(1,128)} %gain_in.1, ...), custom_call_target="tpu_custom_call" | custom-call | tf_op jit(solution)/shard_map/pallas_call | solution.py:630
  173.3 1.6 copy.13

commit v3 on v2

v3 whole, which is shorter than its diff:
```python
import math

import jax
import jax.numpy as jnp
import numpy as np
from jax import lax
from jax.experimental import pallas as pl
from jax.experimental.pallas import tpu as pltpu
from jax.sharding import PartitionSpec as P

HEAD_DIM = 128
ROPE_THETA = 500000.0
NORM_EPSILON = 1e-05
MESH = pl.DeviceIdType.MESH

LAYERS = 4
NZ, NX, NY = 8, 4, 4
SEQ = 64
WIDTH = 4096
CHUNK = 128
SET = NZ * CHUNK
QKV = 1536
HEADS = 1024
GROUP = QKV // 2
EXTRA = GROUP + 128
STREAM = 2 * SEQ
HALF = HEADS // 2
TOK = NX * SEQ
PIECE = SET // NY
PIECES = (4, 2)


TWO_PI_HIGH = 6.28125
TWO_PI_MID = 0.0019340515136718750
TWO_PI_LOW = 2 * math.pi - TWO_PI_HIGH - TWO_PI_MID
SINE_TERMS = [(-1.0) ** k / math.factorial(2 * k + 1) for k in range(10)]
COSINE_TERMS = [(-1.0) ** k / math.factorial(2 * k) for k in range(11)]


def frequencies():
    half = HEAD_DIM // 2
    table = np.float64(ROPE_THETA) ** (-np.arange(half, dtype=np.float64) / half)
    return np.tile(table.astype(np.float32), 2)[None, :].repeat(8, axis=0)


def series(terms, square):
    total = jnp.full(square.shape, terms[-1], jnp.float32)
    for term in terms[-2::-1]:
        total = total * square + term
    return total


def sine_and_cosine(angle):
    turns = jnp.floor(angle * (0.5 / math.pi) + 0.5)
    rest = ((angle - turns * TWO_PI_HIGH) - turns * TWO_PI_MID) - turns * TWO_PI_LOW
    square = rest * rest
    return rest * series(SINE_TERMS, square), series(COSINE_TERMS, square)


def stack_kernel(
    order,
    boundary,
    offset,
    lengths,
    tokens,
    freq,
    gain_in,
    wq,
    wk,
    wv,
    wo,
    out,
    wqkv,
    wob,
    gbuf,
    tsend,
    xbuf,
    xg,
    psend,
    precv,
    abuf,
    osend,
    oown,
    orecv,
    frecv,
    tok_v,
    freq_v,
    gain,
    tables,
    isem,
    lsem,
    hop_sq,
    hop_rq,
    hop_so,
    hop_ro,
    own_s,
    own_r,
    par_sq,
    par_rq,
    par_so,
    par_ro,
    g_s,
    g_r,
    t_s,
    t_r,
    tab_s,
    tab_r,
    x_s,
    x_r,
    p_s,
    p_r,
    a_s,
    a_r,
    o_s,
    o_r,
    f_s,
    f_r,
):
    dp = lax.axis_index("dp")
    p = lax.axis_index("pipe")
    y = lax.axis_index("tensor")
    z = dp // NX
    x = dp % NX
    step = 1 - 2 * p

    def at(zz, xx, pp, yy):
        return {"dp": zz * NX + xx, "pipe": pp, "tensor": yy}

    def zrel(k):
        return (z + step * k + NZ) % NZ

    down = at(zrel(1), x, p, y)
    up = at(zrel(-1), x, p, y)
    other = at(z, x, 1 - p, y)

    def remote(src, dst, s, r, dev):
        return pltpu.make_async_remote_copy(
            src_ref=src, dst_ref=dst, send_sem=s, recv_sem=r, device_id=dev, device_id_type=MESH
        )

    def layer_of(d):
        return p + d * (3 - 2 * p)

    def rows_of(zz):
        return pl.ds(pl.multiple_of(zz * CHUNK, CHUNK), CHUNK)

    def loads(d):
        c = layer_of(d)
        r = rows_of(z)
        copies = []
        for g in range(2):
            for k, (source, width, first) in enumerate(
                ((wq, 512, 0), (wk, 128, 512), (wv, 128, 640))
            ):
                copies.append(
                    pltpu.make_async_copy(
                        source.at[d, 0, :, pl.ds(g * width, width)],
                        wqkv.at[c, r, pl.ds(g * GROUP + first, width)],
                        lsem.at[d, g * 3 + k],
                    )
                )
        copies.append(pltpu.make_async_copy(wo.at[d, 0], wob.at[c, :, r], lsem.at[d, 6]))
        return copies

    small = [
        pltpu.make_async_copy(tokens, tok_v, isem.at[0]),
        pltpu.make_async_copy(freq, freq_v, isem.at[1]),
        pltpu.make_async_copy(gain_in, gain, isem.at[2]),
    ]
    for copy in loads(0) + small + loads(1):
        copy.start()

    barrier = pltpu.get_barrier_semaphore()
    peers = [down, up, other]
    for i in (1, 2, 3):
        peers.append(at(z, (x + i) % NX, p, y))
        peers.append(at(z, (x + i) % NX, 1 - p, y))
        peers.append(at(z, x, p, (y + i) % NY))
    for dev in peers:
        pl.semaphore_signal(barrier, inc=1, device_id=dev, device_id_type=MESH)
    pl.semaphore_wait(barrier, len(peers))

    def piece(c, zz, t, k):
        rows = (CHUNK if t == 0 else HEADS) // PIECES[t]
        if t == 0:
            return wqkv.at[c, pl.ds(pl.multiple_of(zz * CHUNK + k * rows, rows), rows), :]
        return wob.at[c, pl.ds(pl.multiple_of(k * rows, rows), rows), rows_of(zz)]

    def whole(c, zz, t):
        if t == 0:
            return wqkv.at[c, rows_of(zz), :]
        return wob.at[c, :, rows_of(zz)]

    hop_s, hop_r, par_s, par_r = (hop_sq, hop_so), (hop_rq, hop_ro), (par_sq, par_so), (par_rq, par_ro)

    def hop_out(c, t, k, h):
        ref = piece(c, zrel(1 - h), t, k)
        return remote(ref, ref, hop_s[t].at[c, k, h - 1], hop_r[t].at[c, k, h - 1], down)

    def hop_in(c, t, k, h):
        ref = piece(c, zrel(-h), t, k)
        return remote(ref, ref, hop_s[t].at[c, k, h - 1], hop_r[t].at[c, k, h - 1], up)

    def swap_out(c, t, k, h):
        ref = piece(c, zrel(-h), t, k)
        return remote(ref, ref, par_s[t].at[c, k, h - 1], par_r[t].at[c, k, h - 1], other)

    def swap_in(c, t, k, h):
        ref = piece(c, zrel(h), t, k)
        return remote(ref, ref, par_s[t].at[c, k, h - 1], par_r[t].at[c, k, h - 1], other)

    def own_swap(c, t):
        ref = whole(c, z, t)
        return remote(ref, ref, own_s.at[c, t], own_r.at[c, t], other)

    def holder(c):
        return jnp.where((c == 0) | (c == 3), 0, 1)

    def nth(t, j, core):
        return (j + core * (PIECES[t] // 2)) % PIECES[t]

    def first_hop(c, t):
        @pl.when(p != holder(c))
        def _():
            own_swap(c, t).wait_recv()

        for j in range(PIECES[t]):
            hop_out(c, t, nth(t, j, p), 1).start()

    def forward(c, t, h):
        for j in range(PIECES[t]):
            k = nth(t, j, p)
            hop_in(c, t, k, h).wait_recv()
            if h < 3 or j < PIECES[t] // 2:
                hop_out(c, t, k, h + 1).start()
            swap_out(c, t, k, h).start()

    def finish(c, t):
        for j in range(PIECES[t] // 2):
            k = nth(t, j, p)
            hop_in(c, t, k, 4).wait_recv()
            swap_out(c, t, k, 4).start()

    def ready(c, t):
        for h in (1, 2, 3):
            for k in range(PIECES[t]):
                swap_in(c, t, k, h).wait_recv()
        for j in range(PIECES[t] // 2):
            swap_in(c, t, nth(t, j, 1 - p), 4).wait_recv()

    def load_and_share(d):
        copies = loads(d)
        for t in range(2):
            for copy in (copies[:6], copies[6:])[t]:
                copy.wait()
            own_swap(layer_of(d), t).start()

    load_and_share(0)
    first_hop(0, 0)

    for copy in small:
        copy.wait()
    second = order[0, p] == 1

    def chosen(first, other_one):
        return jnp.where(second, other_one, first)

    for xx in range(NX):
        for k in range(2):
            cols = slice(k * 512 + xx * 128, k * 512 + xx * 128 + 128)
            tsend[xx, :, k * 128 : k * 128 + 128] = chosen(
                tok_v[0, :, cols].astype(jnp.float32), tok_v[1, :, cols].astype(jnp.float32)
            ).astype(jnp.bfloat16)

    def block(ref, b, size):
        return ref.at[pl.ds(pl.multiple_of(b * size, size), size), :]

    def tok_out(i):
        xx = (x + i) % NX
        return remote(
            tsend.at[xx], block(xbuf.at[0, y], x, SEQ), t_s.at[xx], t_r.at[x], at(z, xx, p, y)
        )

    def tok_in(i):
        xx = (x + i) % NX
        return remote(
            tsend.at[xx], block(xbuf.at[0, y], xx, SEQ), t_s.at[xx], t_r.at[xx], at(z, xx, p, y)
        )

    for i in (2, 1, 3):
        tok_out(i).start()
    xbuf[0, y, pl.ds(pl.multiple_of(x * SEQ, SEQ), SEQ), :] = tsend[x]

    forward(0, 0, 1)
    load_and_share(1)

    for d in range(2):
        c = layer_of(d)
        for zz in range(NZ):
            row = gain[d, :, pl.ds(pl.multiple_of((zz * NX + x) * CHUNK, CHUNK), CHUNK)]
            gbuf[c, :, zz * CHUNK : zz * CHUNK + CHUNK] = jnp.broadcast_to(row, (8, CHUNK))

    def gain_swap(d, c):
        return remote(gbuf.at[c], gbuf.at[c], g_s.at[d], g_r.at[d], other)

    for d in range(2):
        gain_swap(d, layer_of(d)).start()

    def stream_rows(st):
        return pl.ds(st * STREAM, STREAM)

    def stream_out(c, st, i):
        yy = (y + i) % NY
        ref = xbuf.at[c, y, stream_rows(st), :]
        return remote(ref, ref, x_s.at[c, st, yy], x_r.at[c, st, y], at(z, x, p, yy))

    def stream_in(c, st, i):
        yy = (y + i) % NY
        ref = xbuf.at[c, yy, stream_rows(st), :]
        return remote(ref, ref, x_s.at[c, st, yy], x_r.at[c, st, yy], at(z, x, p, yy))

    for i in (2, 1, 3):
        tok_in(i).wait_recv()
    for st in range(2):
        for i in (2, 1, 3):
            stream_out(0, st, i).start()

    row = lax.broadcasted_iota(jnp.int32, (SEQ, 128), 0)
    lane = lax.broadcasted_iota(jnp.int32, (SEQ, 128), 1)
    cut = chosen(boundary[0], boundary[1])
    jump = chosen(offset[0], offset[1])
    places = jnp.where(row < cut, row, row + jump)
    sine, cosine = sine_and_cosine(places.astype(jnp.float32) * freq_v[0:1, :])
    tables[x, 0] = cosine
    tables[x, 1] = jnp.where(lane < 64, -sine, sine)
    end = 0
    doc_from = jnp.zeros((SEQ, 128), jnp.int32)
    doc_to = jnp.zeros((SEQ, 128), jnp.int32)
    for k in range(4):
        end = end + chosen(lengths[0, k], lengths[1, k])
        doc_from = doc_from + jnp.where(row >= end, 1, 0)
        doc_to = doc_to + jnp.where(lane >= end, 1, 0)
    allowed = (doc_from == doc_to) & (lane <= row)
    tables[x, 2] = jnp.where(allowed, 0.0, -jnp.inf).astype(jnp.float32)

    def table_out(i):
        xx = (x + i) % NX
        return remote(tables.at[x], tables.at[x], tab_s.at[xx], tab_r.at[x], at(z, xx, p, y))

    def table_in(i):
        xx = (x + i) % NX
        return remote(tables.at[xx], tables.at[xx], tab_s.at[xx], tab_r.at[xx], at(z, xx, p, y))

    for i in (2, 1, 3):
        table_out(i).start()

    forward(0, 0, 2)
    forward(0, 0, 3)
    first_hop(0, 1)
    first_hop(1, 0)
    first_hop(1, 1)
    finish(0, 0)
    for d in range(2):
        gain_swap(d, 1 - p + d * (1 + 2 * p)).wait_recv()
    for i in (2, 1, 3):
        table_in(i).wait_recv()

    def part_out(c, st, xx):
        return remote(
            psend.at[st, xx],
            precv.at[c, st, x],
            p_s.at[st, xx],
            p_r.at[c, st, x],
            at(z, xx, p, y),
        )

    def part_in(c, st, i):
        xx = (x + i) % NX
        return remote(
            psend.at[st, xx],
            precv.at[c, st, xx],
            p_s.at[st, xx],
            p_r.at[c, st, xx],
            at(z, xx, p, y),
        )

    def attn_ref(c, st, xx):
        return abuf.at[c, st, xx % 2, xx // 2]

    def attn_out(c, st, i):
        xx = (x + i) % NX
        ref = attn_ref(c, st, x)
        return remote(ref, ref, a_s.at[st, xx], a_r.at[c, st, x], at(z, xx, p, y))

    def attn_in(c, st, i):
        xx = (x + i) % NX
        ref = attn_ref(c, st, xx)
        return remote(ref, ref, a_s.at[st, xx], a_r.at[c, st, xx], at(z, xx, p, y))

    def proj_out(c, st, yy):
        return remote(
            osend.at[st, yy], orecv.at[c, st, y], o_s.at[st, yy], o_r.at[c, st, y], at(z, x, p, yy)
        )

    def proj_in(c, st, yy):
        return remote(
            osend.at[st, yy], orecv.at[c, st, yy], o_s.at[st, yy], o_r.at[c, st, yy], at(z, x, p, yy)
        )

    def project_stage(c, st):
        for i in (1, 3, 2):
            attn_in(c, st, i).wait_recv()
        for xx in range(NX):

            @pl.when(xx != x)
            def _():
                part_out(c, st, xx).wait_send()

        def proj(yy):
            cols = pl.ds(pl.multiple_of(yy * PIECE, PIECE), PIECE)
            total = jnp.zeros((STREAM, PIECE), jnp.float32)
            for g in range(2):
                total = total + jnp.dot(
                    abuf[c, st, g].reshape(STREAM, HALF),
                    wob[c, g * HALF : g * HALF + HALF, cols],
                    preferred_element_type=jnp.float32,
                )
            return total

        def proj_tile(i, carry):
            yy = (y + i) % NY
            osend[st, yy] = proj(yy).astype(jnp.bfloat16)
            proj_out(c, st, yy).start()
            return carry

        lax.fori_loop(1, NY, proj_tile, 0)
        oown[st] = proj(y)

    def add_stage(c, st):
        for i in (1, 3, 2):
            proj_in(c, st, (y + i) % NY).wait_recv()
        for i in (1, 2, 3):
            proj_out(c, st, (y + i) % NY).wait_send()
            attn_out(c, st, i).wait_send()
        for b in range(2):
            rows = slice(b * SEQ, b * SEQ + SEQ)
            places = slice(st * STREAM + b * SEQ, st * STREAM + b * SEQ + SEQ)
            total = oown[st, rows, :]
            for i in (1, 2, 3):
                total = total + orecv[c, st, (y + i) % NY, rows, :].astype(jnp.float32)
            total = total + xbuf[c, y, places, :].astype(jnp.float32)
            xbuf[c + 1, y, places, :] = total.astype(jnp.bfloat16)

        @pl.when(c < LAYERS - 1)
        def _():
            for i in (2, 1, 3):
                stream_out(c + 1, st, i).start()

    def qkv_stage(c, st):
        for i in (1, 3, 2):
            stream_in(c, st, i).wait_recv()
        for b in range(2):
            rows = slice(b * SEQ, b * SEQ + SEQ)
            places = slice(st * STREAM + b * SEQ, st * STREAM + b * SEQ + SEQ)
            total = jnp.zeros((SEQ, 1), jnp.float32)
            for yy in range(NY):
                wide = xbuf[c, yy, places, :].astype(jnp.float32)
                total = total + jnp.sum(wide * wide, axis=1, keepdims=True)
                gains = gbuf[c, 0:1, yy * PIECE : yy * PIECE + PIECE]
                xg[yy, rows, :] = (wide * gains).astype(jnp.bfloat16)
            high = total.astype(jnp.bfloat16).astype(jnp.float32)
            mixed = jnp.where(lane == 0, high, jnp.where(lane == 1, total - high, 0.0))
            for g in range(2):
                psend[st, b * 2 + g, :, GROUP:EXTRA] = mixed.astype(jnp.bfloat16)
        if st == 0:
            ready(c, 0)
        for g in range(2):

            def qkv_tile(n, carry):
                cols = pl.ds(pl.multiple_of(g * GROUP + n * 256, 256), 256)
                acc = jnp.zeros((STREAM, 256), jnp.float32)
                for yy in range(NY):
                    acc = acc + jnp.dot(
                        xg[yy],
                        wqkv[c, yy * PIECE : yy * PIECE + PIECE, cols],
                        preferred_element_type=jnp.float32,
                    )
                acc = acc.astype(jnp.bfloat16)
                for b in range(2):
                    psend[st, b * 2 + g, :, pl.ds(pl.multiple_of(n * 256, 256), 256)] = acc[
                        b * SEQ : b * SEQ + SEQ
                    ]
                return carry

            lax.fori_loop(0, GROUP // 256, qkv_tile, 0)
            for b in range(2):

                @pl.when(b * 2 + g != x)
                def _():
                    part_out(c, st, b * 2 + g).start()

    def attention_stage(c, st):
        for i in (1, 3, 2):
            part_in(c, st, i).wait_recv()
        for i in (1, 2, 3):
            stream_out(c, st, i).wait_send()
        mine = st * 2 + x // 2

        def summed(b):
            cols = slice(b * 128, b * 128 + 128)
            total = psend[st, x, :, cols].astype(jnp.float32)
            for i in (1, 2, 3):
                total = total + precv[c, st, (x + i) % NX, :, cols].astype(jnp.float32)
            return total

        square = jnp.sum(summed(6), axis=1, keepdims=True)
        inv_rms = lax.rsqrt(square * (1.0 / WIDTH) + NORM_EPSILON)

        def turned(b):
            value = summed(b) * inv_rms
            return (value * tables[mine, 0] + pltpu.roll(value, 64, 1) * tables[mine, 1]).astype(
                jnp.bfloat16
            )

        keys = turned(4)
        vals = (summed(5) * inv_rms).astype(jnp.bfloat16)
        query = jnp.concatenate([turned(j) for j in range(4)], axis=0)
        scores = lax.dot_general(
            query, keys, (((1,), (1,)), ((), ())), preferred_element_type=jnp.float32
        )
        bias = jnp.concatenate([tables[mine, 2, :, 0:SEQ]] * 4, axis=0)
        scores = scores * HEAD_DIM ** (-0.5) + bias
        top = jnp.max(scores, axis=1, keepdims=True)
        expo = jnp.exp(scores - top)
        weights = (expo / jnp.sum(expo, axis=1, keepdims=True)).astype(jnp.bfloat16)
        mixed = jnp.dot(weights, vals, preferred_element_type=jnp.float32).astype(jnp.bfloat16)
        for j in range(4):
            abuf[c, st, x % 2, x // 2, :, j * 128 : j * 128 + 128] = mixed[j * SEQ : j * SEQ + SEQ]
        for i in (2, 1, 3):
            attn_out(c, st, i).start()

    def only(condition, *events):
        @pl.when(condition)
        def _():
            for event in events:
                event()

    def layer(c, carry):
        later = c > 0
        next1 = later & (c < LAYERS - 1)
        next2 = later & (c < LAYERS - 2)

        only(later, lambda: forward(c, 1, 3))
        qkv_stage(c, 0)

        only(next1, lambda: forward(c + 1, 0, 2))
        only(later, lambda: project_stage(c - 1, 1))

        only(next1, lambda: forward(c + 1, 1, 1))
        only(
            c == 0,
            lambda: forward(c, 1, 1),
            lambda: forward(c + 1, 0, 1),
            lambda: forward(c, 1, 2),
        )
        attention_stage(c, 0)

        only(later, lambda: finish(c, 1))
        only(next2, lambda: first_hop(c + 2, 0))
        only(later, lambda: add_stage(c - 1, 1))

        only(next1, lambda: forward(c + 1, 0, 3))
        only(
            c == 0,
            lambda: forward(c, 1, 3),
            lambda: forward(c + 1, 0, 2),
            lambda: finish(c, 1),
        )
        ready(c, 1)
        project_stage(c, 0)

        only(next1, lambda: forward(c + 1, 1, 2))
        only(c == 0, lambda: forward(c + 1, 1, 1), lambda: first_hop(c + 2, 0))
        qkv_stage(c, 1)

        only(next2, lambda: forward(c + 2, 0, 1))
        only(c == 0, lambda: forward(c + 1, 0, 3), lambda: forward(c + 1, 1, 2))
        add_stage(c, 0)

        only(next1, lambda: finish(c + 1, 0))
        only(next2, lambda: first_hop(c + 2, 1))
        only(
            c == 0,
            lambda: forward(c + 2, 0, 1),
            lambda: finish(c + 1, 0),
            lambda: first_hop(c + 2, 1),
        )
        attention_stage(c, 1)
        return carry

    lax.fori_loop(0, LAYERS, layer, 0)
    project_stage(LAYERS - 1, 1)
    add_stage(LAYERS - 1, 1)

    def done_rows(xx, q):
        return pl.ds(pl.multiple_of(xx * SEQ + q * 32, 32), 32)

    def done_out(i, j):
        xx, q = (x + i) % NX, (p + j) % 2
        return remote(
            xbuf.at[LAYERS, y, done_rows(xx, q), :],
            frecv.at[p, x],
            f_s.at[q, xx],
            f_r.at[p, x],
            at(z, xx, q, y),
        )

    def done_in(i, j):
        xx, q = (x + i) % NX, (p + j) % 2
        return remote(
            xbuf.at[LAYERS, y, done_rows(xx, q), :],
            frecv.at[q, xx],
            f_s.at[q, xx],
            f_r.at[q, xx],
            at(z, xx, q, y),
        )

    away = [(i, j) for i in (2, 1, 3, 0) for j in range(2) if (i, j) != (0, 0)]
    for i, j in away:
        done_out(i, j).start()
    frecv[p, x] = xbuf[LAYERS, y, done_rows(x, p), :]
    for i, j in away:
        done_in(i, j).wait_recv()
    for q in range(2):
        for xx in range(NX):
            out[q, :, xx * 128 : xx * 128 + 128] = frecv[q, xx, :, 0:128]
            out[q, :, 512 + xx * 128 : 512 + xx * 128 + 128] = frecv[q, xx, :, 128:256]

    for i, j in away:
        done_out(i, j).wait_send()
    for i in (1, 2, 3):
        tok_out(i).wait_send()
        table_out(i).wait_send()
    for d in range(2):
        gain_swap(d, layer_of(d)).wait_send()
        for t in range(2):
            own_swap(layer_of(d), t).wait_send()

    def drain(c, carry):
        for t in range(2):
            for k in range(PIECES[t]):
                for h in (1, 2, 3):
                    hop_out(c, t, k, h).wait_send()
                    swap_out(c, t, k, h).wait_send()
            for j in range(PIECES[t] // 2):
                hop_out(c, t, nth(t, j, p), 4).wait_send()
                swap_out(c, t, nth(t, j, p), 4).wait_send()

        return carry

    lax.fori_loop(0, LAYERS, drain, 0)


def per_device(
    tokens,
    w_query,
    w_key,
    w_value,
    w_out,
    norm_gain,
    boundary,
    skip_offset,
    doc_lengths,
    batch_order,
):
    vmem = pl.BlockSpec(memory_space=pltpu.VMEM)
    smem = pl.BlockSpec(memory_space=pltpu.SMEM)
    anywhere = pl.BlockSpec(memory_space=pl.ANY)
    dma = pltpu.SemaphoreType.DMA
    bf16, f32 = jnp.bfloat16, jnp.float32
    return pl.pallas_call(
        stack_kernel,
        out_shape=jax.ShapeDtypeStruct((2, 32, 1024), bf16),
        in_specs=[smem] * 4 + [anywhere] * 7,
        out_specs=vmem,
        scratch_shapes=[
            pltpu.VMEM((LAYERS, SET, QKV), bf16),
            pltpu.VMEM((LAYERS, HEADS, SET), bf16),
            pltpu.VMEM((LAYERS, 8, SET), f32),
            pltpu.VMEM((NX, SEQ, PIECE), bf16),
            pltpu.VMEM((LAYERS + 1, NY, TOK, PIECE), bf16),
            pltpu.VMEM((NY, STREAM, PIECE), bf16),
            pltpu.VMEM((2, NX, SEQ, EXTRA), bf16),
            pltpu.VMEM((LAYERS, 2, NX, SEQ, EXTRA), bf16),
            pltpu.VMEM((LAYERS, 2, 2, 2, SEQ, HALF), bf16),
            pltpu.VMEM((2, NY, STREAM, PIECE), bf16),
            pltpu.VMEM((2, STREAM, PIECE), f32),
            pltpu.VMEM((LAYERS, 2, NY, STREAM, PIECE), bf16),
            pltpu.VMEM((2, NX, 32, PIECE), bf16),
            pltpu.VMEM((2, SEQ, 1024), bf16),
            pltpu.VMEM((8, HEAD_DIM), f32),
            pltpu.VMEM((2, 1, WIDTH), f32),
            pltpu.VMEM((NX, 3, SEQ, HEAD_DIM), f32),
            dma((3,)),
            dma((2, 7)),
            dma((LAYERS, PIECES[0], 4)),
            dma((LAYERS, PIECES[0], 4)),
            dma((LAYERS, PIECES[1], 4)),
            dma((LAYERS, PIECES[1], 4)),
            dma((LAYERS, 2)),
            dma((LAYERS, 2)),
            dma((LAYERS, PIECES[0], 4)),
            dma((LAYERS, PIECES[0], 4)),
            dma((LAYERS, PIECES[1], 4)),
            dma((LAYERS, PIECES[1], 4)),
            dma((2,)),
            dma((2,)),
            dma((NX,)),
            dma((NX,)),
            dma((NX,)),
            dma((NX,)),
            dma((LAYERS, 2, NY)),
            dma((LAYERS, 2, NY)),
            dma((2, NX)),
            dma((LAYERS, 2, NX)),
            dma((2, NX)),
            dma((LAYERS, 2, NX)),
            dma((2, NY)),
            dma((LAYERS, 2, NY)),
            dma((2, NX)),
            dma((2, NX)),
        ],
        compiler_params=pltpu.CompilerParams(
            collective_id=0, has_side_effects=True, vmem_limit_bytes=60 * 1024 * 1024
        ),
    )(
        batch_order,
        boundary,
        skip_offset,
        doc_lengths,
        tokens,
        jnp.asarray(frequencies()),
        norm_gain,
        w_query,
        w_key,
        w_value,
        w_out,
    )


def solution(mesh):
    placed = (
        P("dp", None, "tensor"),
        P(None, "pipe", "dp", "tensor"),
        P(None, "pipe", "dp", "tensor"),
        P(None, "pipe", "dp", "tensor"),
        P(None, "pipe", "tensor", "dp"),
        P(None, "pipe", None),
        P("dp"),
        P("dp"),
        P("dp", None),
        P("dp", None),
    )
    return jax.shard_map(
        per_device, mesh=mesh, in_specs=placed, out_specs=P("dp", "pipe", "tensor"), check_vma=False
    )
```

time: 175 us -> 164 us (0.937)
  Pallas kernels: 173 us -> 162 us
    pallas_call x1, Pallas kernels: 173 us -> 162 us  [per_device(): pl.pallas_call(stack_kernel, out_shape=jax.ShapeDtypeStruct((2, 32, 1024)...]
where the time goes in v3:
time: 164 us
  Pallas kernels  162 us (99%)
    pallas_call x1, Pallas kernels, per_device(): pl.pallas_call(stack_kernel, out_shape=jax.ShapeDtypeStruct((2, 32, 1024)...  162 us

profile of v3, /device:TPU:1, one launch (start us, length us, event | category | flops | bytes accessed | tf_op | source)
XLA Modules:
  0.0 163.8 jit_solution(5512737589270700888)
XLA Ops:
  0.0 162.3 %shard_map.109 = bf16[2,32,1024]{2,1,0:T(8,128)(2,1)} custom-call(s32[1,2]{1,0:T(1,128)} %order.1, s32[2]{0:T(128)} %boundary.1, s32[2]{0:T(128)} %offset.1, s32[2,4]{1,0:T(2,128)} %lengths.1, bf16[2,64,1024]{2,1,0:T(8,128)(2,1)} %tokens.1, f32[8,128]{1,0:T(8,128)} %constant.2.clone.freq, f32[2,1,4096]{2,1,0:T(1,128)} %gain_in.1, ...), custom_call_target="tpu_custom_call" | custom-call | tf_op jit(solution)/shard_map/pallas_call | solution.py:681
  162.3 1.6 copy.13

commit v4 on v3

--- a/solution.py
+++ b/solution.py
@@ -22,7 +22,6 @@
 QKV = 1536
 HEADS = 1024
 GROUP = QKV // 2
-EXTRA = GROUP + 128
 STREAM = 2 * SEQ
 HALF = HEADS // 2
 TOK = NX * SEQ
@@ -55,6 +54,51 @@
     rest = ((angle - turns * TWO_PI_HIGH) - turns * TWO_PI_MID) - turns * TWO_PI_LOW
     square = rest * rest
     return rest * series(SINE_TERMS, square), series(COSINE_TERMS, square)
+
+
+PROLOGUE = ((0, 1, 0), (0, 1, 1), (0, 0, 4), (1, 0, 0))
+EVENTS = (
+    (
+        (),
+        ((0, 1, 2),),
+        ((1, 0, 1), (0, 1, 3)),
+        (),
+        ((1, 0, 2), (1, 1, 0), (0, 1, 4)),
+        (),
+        ((1, 0, 3), (1, 1, 1)),
+        ((2, 0, 0), (1, 0, 4)),
+    ),
+    (
+        ((1, 1, 2),),
+        ((2, 0, 1),),
+        (),
+        ((1, 1, 3), (2, 1, 0)),
+        ((1, 1, 4), (2, 0, 2)),
+        (),
+        ((2, 0, 3), (2, 1, 1)),
+        ((3, 0, 0), (2, 0, 4)),
+    ),
+    (
+        (),
+        ((2, 1, 2),),
+        ((3, 1, 0), (2, 1, 3), (3, 0, 1)),
+        (),
+        ((2, 1, 4),),
+        ((3, 0, 2),),
+        (),
+        ((3, 0, 3), (3, 1, 1)),
+    ),
+    (
+        ((3, 0, 4),),
+        ((3, 1, 2),),
+        ((3, 1, 3),),
+        ((3, 1, 4),),
+        (),
+        (),
+        (),
+        (),
+    ),
+)
 
 
 def stack_kernel(
@@ -78,6 +122,8 @@
     xg,
     psend,
     precv,
+    qsend,
+    qrecv,
     abuf,
     osend,
     oown,
@@ -93,8 +139,10 @@
     hop_rq,
     hop_so,
     hop_ro,
-    own_s,
-    own_r,
+    own_sq,
+    own_rq,
+    own_so,
+    own_ro,
     par_sq,
     par_rq,
     par_so,
@@ -109,6 +157,8 @@
     x_r,
     p_s,
     p_r,
+    q_s,
+    q_r,
     a_s,
     a_r,
     o_s,
@@ -162,14 +212,6 @@
         copies.append(pltpu.make_async_copy(wo.at[d, 0], wob.at[c, :, r], lsem.at[d, 6]))
         return copies
 
-    small = [
-        pltpu.make_async_copy(tokens, tok_v, isem.at[0]),
-        pltpu.make_async_copy(freq, freq_v, isem.at[1]),
-        pltpu.make_async_copy(gain_in, gain, isem.at[2]),
-    ]
-    for copy in loads(0) + small + loads(1):
-        copy.start()
-
     barrier = pltpu.get_barrier_semaphore()
     peers = [down, up, other]
     for i in (1, 2, 3):
@@ -178,6 +220,14 @@
         peers.append(at(z, x, p, (y + i) % NY))
     for dev in peers:
         pl.semaphore_signal(barrier, inc=1, device_id=dev, device_id_type=MESH)
+
+    small = [
+        pltpu.make_async_copy(tokens, tok_v, isem.at[0]),
+        pltpu.make_async_copy(freq, freq_v, isem.at[1]),
+        pltpu.make_async_copy(gain_in, gain, isem.at[2]),
+    ]
+    for copy in loads(0) + small + loads(1):
+        copy.start()
     pl.semaphore_wait(barrier, len(peers))
 
     def piece(c, zz, t, k):
@@ -186,12 +236,9 @@
             return wqkv.at[c, pl.ds(pl.multiple_of(zz * CHUNK + k * rows, rows), rows), :]
         return wob.at[c, pl.ds(pl.multiple_of(k * rows, rows), rows), rows_of(zz)]
 
-    def whole(c, zz, t):
-        if t == 0:
-            return wqkv.at[c, rows_of(zz), :]
-        return wob.at[c, :, rows_of(zz)]
-
-    hop_s, hop_r, par_s, par_r = (hop_sq, hop_so), (hop_rq, hop_ro), (par_sq, par_so), (par_rq, par_ro)
+    hop_s, hop_r = (hop_sq, hop_so), (hop_rq, hop_ro)
+    par_s, par_r = (par_sq, par_so), (par_rq, par_ro)
+    own_s, own_r = (own_sq, own_so), (own_rq, own_ro)
 
     def hop_out(c, t, k, h):
         ref = piece(c, zrel(1 - h), t, k)
@@ -209,9 +256,9 @@
         ref = piece(c, zrel(h), t, k)
         return remote(ref, ref, par_s[t].at[c, k, h - 1], par_r[t].at[c, k, h - 1], other)
 
-    def own_swap(c, t):
-        ref = whole(c, z, t)
-        return remote(ref, ref, own_s.at[c, t], own_r.at[c, t], other)
+    def own_swap(c, t, k):
+        ref = piece(c, z, t, k)
+        return remote(ref, ref, own_s[t].at[c, k], own_r[t].at[c, k], other)
 
     def holder(c):
         return jnp.where((c == 0) | (c == 3), 0, 1)
@@ -220,12 +267,14 @@
         return (j + core * (PIECES[t] // 2)) % PIECES[t]
 
     def first_hop(c, t):
-        @pl.when(p != holder(c))
-        def _():
-            own_swap(c, t).wait_recv()
-
         for j in range(PIECES[t]):
-            hop_out(c, t, nth(t, j, p), 1).start()
+            k = nth(t, j, p)
+
+            @pl.when(p != holder(c))
+            def _():
+                own_swap(c, t, k).wait_recv()
+
+            hop_out(c, t, k, 1).start()
 
     def forward(c, t, h):
         for j in range(PIECES[t]):
@@ -253,10 +302,20 @@
         for t in range(2):
             for copy in (copies[:6], copies[6:])[t]:
                 copy.wait()
-            own_swap(layer_of(d), t).start()
+            for j in range(PIECES[t]):
+                own_swap(layer_of(d), t, nth(t, j, 1 - p)).start()
 
     load_and_share(0)
     first_hop(0, 0)
+
+    def run(event):
+        c, t, h = event
+        if h == 0:
+            first_hop(c, t)
+        elif h < 4:
+            forward(c, t, h)
+        else:
+            finish(c, t)
 
     for copy in small:
         copy.wait()
@@ -356,10 +415,8 @@
 
     forward(0, 0, 2)
     forward(0, 0, 3)
-    first_hop(0, 1)
-    first_hop(1, 0)
-    first_hop(1, 1)
-    finish(0, 0)
+    for event in PROLOGUE:
+        run(event)
     for d in range(2):
         gain_swap(d, 1 - p + d * (1 + 2 * p)).wait_recv()
     for i in (2, 1, 3):
@@ -381,6 +438,26 @@
             precv.at[c, st, xx],
             p_s.at[st, xx],
             p_r.at[c, st, xx],
+            at(z, xx, p, y),
+        )
+
+    def square_out(c, st, i):
+        xx = (x + i) % NX
+        return remote(
+            qsend.at[st, xx // 2],
+            qrecv.at[c, st, x],
+            q_s.at[st, xx],
+            q_r.at[c, st, x],
+            at(z, xx, p, y),
+        )
+
+    def square_in(c, st, i):
+        xx = (x + i) % NX
+        return remote(
+            qsend.at[st, xx // 2],
+            qrecv.at[c, st, xx],
+            q_s.at[st, xx],
+            q_r.at[c, st, xx],
             at(z, xx, p, y),
         )
 
@@ -442,6 +519,7 @@
         for i in (1, 2, 3):
             proj_out(c, st, (y + i) % NY).wait_send()
             attn_out(c, st, i).wait_send()
+            square_out(c, st, i).wait_send()
         for b in range(2):
             rows = slice(b * SEQ, b * SEQ + SEQ)
             places = slice(st * STREAM + b * SEQ, st * STREAM + b * SEQ + SEQ)
@@ -468,10 +546,10 @@
                 total = total + jnp.sum(wide * wide, axis=1, keepdims=True)
                 gains = gbuf[c, 0:1, yy * PIECE : yy * PIECE + PIECE]
                 xg[yy, rows, :] = (wide * gains).astype(jnp.bfloat16)
-            high = total.astype(jnp.bfloat16).astype(jnp.float32)
-            mixed = jnp.where(lane == 0, high, jnp.where(lane == 1, total - high, 0.0))
-            for g in range(2):
-                psend[st, b * 2 + g, :, GROUP:EXTRA] = mixed.astype(jnp.bfloat16)
+            flat = jnp.sum(jnp.where(row == lane, total, 0.0), axis=0, keepdims=True)
+            qsend[st, b] = jnp.broadcast_to(flat, (8, 128))
+        for i in (2, 1, 3):
+            square_out(c, st, i).start()
         if st == 0:
             ready(c, 0)
         for g in range(2):
@@ -501,6 +579,13 @@
 
     def attention_stage(c, st):
         for i in (1, 3, 2):
+            square_in(c, st, i).wait_recv()
+        flat = qsend[st, x // 2]
+        for i in (1, 2, 3):
+            flat = flat + qrecv[c, st, (x + i) % NX]
+        square = jnp.sum(jnp.where(row == lane, flat[0:1, :], 0.0), axis=1, keepdims=True)
+        inv_rms = lax.rsqrt(square * (1.0 / WIDTH) + NORM_EPSILON)
+        for i in (1, 3, 2):
             part_in(c, st, i).wait_recv()
         for i in (1, 2, 3):
             stream_out(c, st, i).wait_send()
@@ -512,9 +597,6 @@
             for i in (1, 2, 3):
                 total = total + precv[c, st, (x + i) % NX, :, cols].astype(jnp.float32)
             return total
-
-        square = jnp.sum(summed(6), axis=1, keepdims=True)
-        inv_rms = lax.rsqrt(square * (1.0 / WIDTH) + NORM_EPSILON)
 
         def turned(b):
             value = summed(b) * inv_rms
@@ -539,68 +621,24 @@
         for i in (2, 1, 3):
             attn_out(c, st, i).start()
 
-    def only(condition, *events):
-        @pl.when(condition)
-        def _():
-            for event in events:
-                event()
+    stages = (qkv_stage, attention_stage, project_stage, add_stage)
 
     def layer(c, carry):
-        later = c > 0
-        next1 = later & (c < LAYERS - 1)
-        next2 = later & (c < LAYERS - 2)
-
-        only(later, lambda: forward(c, 1, 3))
-        qkv_stage(c, 0)
-
-        only(next1, lambda: forward(c + 1, 0, 2))
-        only(later, lambda: project_stage(c - 1, 1))
-
-        only(next1, lambda: forward(c + 1, 1, 1))
-        only(
-            c == 0,
-            lambda: forward(c, 1, 1),
-            lambda: forward(c + 1, 0, 1),
-            lambda: forward(c, 1, 2),
-        )
-        attention_stage(c, 0)
-
-        only(later, lambda: finish(c, 1))
-        only(next2, lambda: first_hop(c + 2, 0))
-        only(later, lambda: add_stage(c - 1, 1))
-
-        only(next1, lambda: forward(c + 1, 0, 3))
-        only(
-            c == 0,
-            lambda: forward(c, 1, 3),
-            lambda: forward(c + 1, 0, 2),
-            lambda: finish(c, 1),
-        )
-        ready(c, 1)
-        project_stage(c, 0)
-
-        only(next1, lambda: forward(c + 1, 1, 2))
-        only(c == 0, lambda: forward(c + 1, 1, 1), lambda: first_hop(c + 2, 0))
-        qkv_stage(c, 1)
-
-        only(next2, lambda: forward(c + 2, 0, 1))
-        only(c == 0, lambda: forward(c + 1, 0, 3), lambda: forward(c + 1, 1, 2))
-        add_stage(c, 0)
-
-        only(next1, lambda: finish(c + 1, 0))
-        only(next2, lambda: first_hop(c + 2, 1))
-        only(
-            c == 0,
-            lambda: forward(c + 2, 0, 1),
-            lambda: finish(c + 1, 0),
-            lambda: first_hop(c + 2, 1),
-        )
-        attention_stage(c, 1)
+        for slot in range(8):
+            for at_layer in range(LAYERS):
+                if EVENTS[at_layer][slot]:
+
+                    @pl.when(c == at_layer)
+                    def _():
+                        for event in EVENTS[at_layer][slot]:
+                            run(event)
+
+            if slot == 4:
+                ready(c, 1)
+            stages[slot // 2](c, slot % 2)
         return carry
 
     lax.fori_loop(0, LAYERS, layer, 0)
-    project_stage(LAYERS - 1, 1)
-    add_stage(LAYERS - 1, 1)
 
     def done_rows(xx, q):
         return pl.ds(pl.multiple_of(xx * SEQ + q * 32, 32), 32)
@@ -644,7 +682,8 @@
     for d in range(2):
         gain_swap(d, layer_of(d)).wait_send()
         for t in range(2):
-            own_swap(layer_of(d), t).wait_send()
+            for k in range(PIECES[t]):
+                own_swap(layer_of(d), t, k).wait_send()
 
     def drain(c, carry):
         for t in range(2):
@@ -690,8 +729,10 @@
             pltpu.VMEM((NX, SEQ, PIECE), bf16),
             pltpu.VMEM((LAYERS + 1, NY, TOK, PIECE), bf16),
             pltpu.VMEM((NY, STREAM, PIECE), bf16),
-            pltpu.VMEM((2, NX, SEQ, EXTRA), bf16),
-            pltpu.VMEM((LAYERS, 2, NX, SEQ, EXTRA), bf16),
+            pltpu.VMEM((2, NX, SEQ, GROUP), bf16),
+            pltpu.VMEM((LAYERS, 2, NX, SEQ, GROUP), bf16),
+            pltpu.VMEM((2, 2, 8, 128), f32),
+            pltpu.VMEM((LAYERS, 2, NX, 8, 128), f32),
             pltpu.VMEM((LAYERS, 2, 2, 2, SEQ, HALF), bf16),
             pltpu.VMEM((2, NY, STREAM, PIECE), bf16),
             pltpu.VMEM((2, STREAM, PIECE), f32),
@@ -707,8 +748,10 @@
             dma((LAYERS, PIECES[0], 4)),
             dma((LAYERS, PIECES[1], 4)),
             dma((LAYERS, PIECES[1], 4)),
-            dma((LAYERS, 2)),
-            dma((LAYERS, 2)),
+            dma((LAYERS, PIECES[0])),
+            dma((LAYERS, PIECES[0])),
+            dma((LAYERS, PIECES[1])),
+            dma((LAYERS, PIECES[1])),
             dma((LAYERS, PIECES[0], 4)),
             dma((LAYERS, PIECES[0], 4)),
             dma((LAYERS, PIECES[1], 4)),
@@ -721,6 +764,8 @@
             dma((NX,)),
             dma((LAYERS, 2, NY)),
             dma((LAYERS, 2, NY)),
+            dma((2, NX)),
+            dma((LAYERS, 2, NX)),
             dma((2, NX)),
             dma((LAYERS, 2, NX)),
             dma((2, NX)),

time: 164 us -> 154 us (0.939)
  Pallas kernels: 162 us -> 152 us
    pallas_call x1, Pallas kernels: 162 us -> 152 us  [per_device(): pl.pallas_call(stack_kernel, out_shape=jax.ShapeDtypeStruct((2, 32, 1024)...]
where the time goes in v4:
time: 154 us; the launch traced here: 153 us
  Pallas kernels  152 us (99%)
  local copies, waits for them, and re-layouts  1.57 us (1%)
    pallas_call x1, Pallas kernels, per_device(): pl.pallas_call(stack_kernel, out_shape=jax.ShapeDtypeStruct((2, 32, 1024)...  152 us

profile of v4, /device:TPU:1, one launch (start us, length us, event | category | flops | bytes accessed | tf_op | source)
XLA Modules:
  0.0 153.5 jit_solution(8395250678548421714)
XLA Ops:
  0.0 151.9 %shard_map.109 = bf16[2,32,1024]{2,1,0:T(8,128)(2,1)} custom-call(s32[1,2]{1,0:T(1,128)} %order.1, s32[2]{0:T(128)} %boundary.1, s32[2]{0:T(128)} %offset.1, s32[2,4]{1,0:T(2,128)} %lengths.1, bf16[2,64,1024]{2,1,0:T(8,128)(2,1)} %tokens.1, f32[8,128]{1,0:T(8,128)} %constant.2.clone.freq, f32[2,1,4096]{2,1,0:T(1,128)} %gain_in.1, ...), custom_call_target="tpu_custom_call" | custom-call | tf_op jit(solution)/shard_map/pallas_call | solution.py:720
  151.9 1.6 %copy.13 = bf16[2,32,1024]{2,1,0:T(8,128)(2,1)} copy(bf16[2,32,1024]{2,1,0:T(8,128)(2,1)} %shard_map.109) | data formatting | bytes 262144

commit v5 on v4

--- a/solution.py
+++ b/solution.py
@@ -135,18 +135,14 @@
     tables,
     isem,
     lsem,
-    hop_sq,
+    hop_s,
     hop_rq,
-    hop_so,
     hop_ro,
-    own_sq,
+    own_s,
     own_rq,
-    own_so,
     own_ro,
-    par_sq,
-    par_rq,
-    par_so,
-    par_ro,
+    par_s,
+    par_r,
     g_s,
     g_r,
     t_s,
@@ -199,17 +195,15 @@
         r = rows_of(z)
         copies = []
         for g in range(2):
-            for k, (source, width, first) in enumerate(
-                ((wq, 512, 0), (wk, 128, 512), (wv, 128, 640))
-            ):
+            for source, width, first in ((wq, 512, 0), (wk, 128, 512), (wv, 128, 640)):
                 copies.append(
                     pltpu.make_async_copy(
                         source.at[d, 0, :, pl.ds(g * width, width)],
                         wqkv.at[c, r, pl.ds(g * GROUP + first, width)],
-                        lsem.at[d, g * 3 + k],
+                        lsem.at[d, 0],
                     )
                 )
-        copies.append(pltpu.make_async_copy(wo.at[d, 0], wob.at[c, :, r], lsem.at[d, 6]))
+        copies.append(pltpu.make_async_copy(wo.at[d, 0], wob.at[c, :, r], lsem.at[d, 1]))
         return copies
 
     barrier = pltpu.get_barrier_semaphore()
@@ -236,29 +230,32 @@
             return wqkv.at[c, pl.ds(pl.multiple_of(zz * CHUNK + k * rows, rows), rows), :]
         return wob.at[c, pl.ds(pl.multiple_of(k * rows, rows), rows), rows_of(zz)]
 
-    hop_s, hop_r = (hop_sq, hop_so), (hop_rq, hop_ro)
-    par_s, par_r = (par_sq, par_so), (par_rq, par_ro)
-    own_s, own_r = (own_sq, own_so), (own_rq, own_ro)
+    hop_r = (hop_rq, hop_ro)
+    own_r = (own_rq, own_ro)
+
+    def whole(c, zz, t):
+        if t == 0:
+            return wqkv.at[c, rows_of(zz), :]
+        return wob.at[c, :, rows_of(zz)]
+
+    def stretch(layers, t):
+        return (wqkv, wob)[t].at[layers, pl.ds(0, 448), :]
 
     def hop_out(c, t, k, h):
         ref = piece(c, zrel(1 - h), t, k)
-        return remote(ref, ref, hop_s[t].at[c, k, h - 1], hop_r[t].at[c, k, h - 1], down)
+        return remote(ref, ref, hop_s.at[t], hop_r[t].at[c, k, h - 1], down)
 
     def hop_in(c, t, k, h):
         ref = piece(c, zrel(-h), t, k)
-        return remote(ref, ref, hop_s[t].at[c, k, h - 1], hop_r[t].at[c, k, h - 1], up)
+        return remote(ref, ref, hop_s.at[t], hop_r[t].at[c, k, h - 1], up)
 
     def swap_out(c, t, k, h):
         ref = piece(c, zrel(-h), t, k)
-        return remote(ref, ref, par_s[t].at[c, k, h - 1], par_r[t].at[c, k, h - 1], other)
-
-    def swap_in(c, t, k, h):
-        ref = piece(c, zrel(h), t, k)
-        return remote(ref, ref, par_s[t].at[c, k, h - 1], par_r[t].at[c, k, h - 1], other)
+        return remote(ref, ref, par_s.at[t], par_r.at[c, t], other)
 
     def own_swap(c, t, k):
         ref = piece(c, z, t, k)
-        return remote(ref, ref, own_s[t].at[c, k], own_r[t].at[c, k], other)
+        return remote(ref, ref, own_s.at[t], own_r[t].at[c // 2, k], other)
 
     def holder(c):
         return jnp.where((c == 0) | (c == 3), 0, 1)
@@ -291,17 +288,13 @@
             swap_out(c, t, k, 4).start()
 
     def ready(c, t):
-        for h in (1, 2, 3):
-            for k in range(PIECES[t]):
-                swap_in(c, t, k, h).wait_recv()
-        for j in range(PIECES[t] // 2):
-            swap_in(c, t, nth(t, j, 1 - p), 4).wait_recv()
+        ref = stretch(c, t)
+        remote(ref, ref, par_s.at[t], par_r.at[c, t], other).wait_recv()
 
     def load_and_share(d):
-        copies = loads(d)
         for t in range(2):
-            for copy in (copies[:6], copies[6:])[t]:
-                copy.wait()
+            landed = whole(layer_of(d), z, t)
+            pltpu.make_async_copy(landed, landed, lsem.at[d, t]).wait()
             for j in range(PIECES[t]):
                 own_swap(layer_of(d), t, nth(t, j, 1 - p)).start()
 
@@ -371,12 +364,12 @@
     def stream_out(c, st, i):
         yy = (y + i) % NY
         ref = xbuf.at[c, y, stream_rows(st), :]
-        return remote(ref, ref, x_s.at[c, st, yy], x_r.at[c, st, y], at(z, x, p, yy))
+        return remote(ref, ref, x_s.at[st, yy], x_r.at[st, y], at(z, x, p, yy))
 
     def stream_in(c, st, i):
         yy = (y + i) % NY
         ref = xbuf.at[c, yy, stream_rows(st), :]
-        return remote(ref, ref, x_s.at[c, st, yy], x_r.at[c, st, yy], at(z, x, p, yy))
+        return remote(ref, ref, x_s.at[st, yy], x_r.at[st, yy], at(z, x, p, yy))
 
     for i in (2, 1, 3):
         tok_in(i).wait_recv()
@@ -427,7 +420,7 @@
             psend.at[st, xx],
             precv.at[c, st, x],
             p_s.at[st, xx],
-            p_r.at[c, st, x],
+            p_r.at[st, x],
             at(z, xx, p, y),
         )
 
@@ -437,7 +430,7 @@
             psend.at[st, xx],
             precv.at[c, st, xx],
             p_s.at[st, xx],
-            p_r.at[c, st, xx],
+            p_r.at[st, xx],
             at(z, xx, p, y),
         )
 
@@ -447,7 +440,7 @@
             qsend.at[st, xx // 2],
             qrecv.at[c, st, x],
             q_s.at[st, xx],
-            q_r.at[c, st, x],
+            q_r.at[st, x],
             at(z, xx, p, y),
         )
 
@@ -457,7 +450,7 @@
             qsend.at[st, xx // 2],
             qrecv.at[c, st, xx],
             q_s.at[st, xx],
-            q_r.at[c, st, xx],
+            q_r.at[st, xx],
             at(z, xx, p, y),
         )
 
@@ -467,21 +460,21 @@
     def attn_out(c, st, i):
         xx = (x + i) % NX
         ref = attn_ref(c, st, x)
-        return remote(ref, ref, a_s.at[st, xx], a_r.at[c, st, x], at(z, xx, p, y))
+        return remote(ref, ref, a_s.at[st, xx], a_r.at[st, x], at(z, xx, p, y))
 
     def attn_in(c, st, i):
         xx = (x + i) % NX
         ref = attn_ref(c, st, xx)
-        return remote(ref, ref, a_s.at[st, xx], a_r.at[c, st, xx], at(z, xx, p, y))
+        return remote(ref, ref, a_s.at[st, xx], a_r.at[st, xx], at(z, xx, p, y))
 
     def proj_out(c, st, yy):
         return remote(
-            osend.at[st, yy], orecv.at[c, st, y], o_s.at[st, yy], o_r.at[c, st, y], at(z, x, p, yy)
+            osend.at[st, yy], orecv.at[c, st, y], o_s.at[st, yy], o_r.at[st, y], at(z, x, p, yy)
         )
 
     def proj_in(c, st, yy):
         return remote(
-            osend.at[st, yy], orecv.at[c, st, yy], o_s.at[st, yy], o_r.at[c, st, yy], at(z, x, p, yy)
+            osend.at[st, yy], orecv.at[c, st, yy], o_s.at[st, yy], o_r.at[st, yy], at(z, x, p, yy)
         )
 
     def project_stage(c, st):
@@ -681,23 +674,13 @@
         table_out(i).wait_send()
     for d in range(2):
         gain_swap(d, layer_of(d)).wait_send()
-        for t in range(2):
-            for k in range(PIECES[t]):
-                own_swap(layer_of(d), t, k).wait_send()
-
-    def drain(c, carry):
-        for t in range(2):
-            for k in range(PIECES[t]):
-                for h in (1, 2, 3):
-                    hop_out(c, t, k, h).wait_send()
-                    swap_out(c, t, k, h).wait_send()
-            for j in range(PIECES[t] // 2):
-                hop_out(c, t, nth(t, j, p), 4).wait_send()
-                swap_out(c, t, nth(t, j, p), 4).wait_send()
-
-        return carry
-
-    lax.fori_loop(0, LAYERS, drain, 0)
+
+    for t in range(2):
+        ref = wqkv.at[0, pl.ds(0, 256), :] if t == 0 else wob.at[0, pl.ds(0, 256), :]
+        remote(ref, ref, own_s.at[t], own_r[t].at[0, 0], other).wait_send()
+        ref = stretch(slice(0, LAYERS), t)
+        remote(ref, ref, hop_s.at[t], hop_r[t].at[0, 0, 0], down).wait_send()
+        remote(ref, ref, par_s.at[t], par_r.at[0, t], other).wait_send()
 
 
 def per_device(
@@ -743,38 +726,19 @@
             pltpu.VMEM((2, 1, WIDTH), f32),
             pltpu.VMEM((NX, 3, SEQ, HEAD_DIM), f32),
             dma((3,)),
-            dma((2, 7)),
-            dma((LAYERS, PIECES[0], 4)),
+            dma((2, 2)),
+            dma((2,)),
             dma((LAYERS, PIECES[0], 4)),
             dma((LAYERS, PIECES[1], 4)),
-            dma((LAYERS, PIECES[1], 4)),
-            dma((LAYERS, PIECES[0])),
-            dma((LAYERS, PIECES[0])),
-            dma((LAYERS, PIECES[1])),
-            dma((LAYERS, PIECES[1])),
-            dma((LAYERS, PIECES[0], 4)),
-            dma((LAYERS, PIECES[0], 4)),
-            dma((LAYERS, PIECES[1], 4)),
-            dma((LAYERS, PIECES[1], 4)),
             dma((2,)),
+            dma((2, PIECES[0])),
+            dma((2, PIECES[1])),
             dma((2,)),
-            dma((NX,)),
-            dma((NX,)),
-            dma((NX,)),
-            dma((NX,)),
-            dma((LAYERS, 2, NY)),
-            dma((LAYERS, 2, NY)),
-            dma((2, NX)),
-            dma((LAYERS, 2, NX)),
-            dma((2, NX)),
-            dma((LAYERS, 2, NX)),
-            dma((2, NX)),
-            dma((LAYERS, 2, NX)),
-            dma((2, NY)),
-            dma((LAYERS, 2, NY)),
-            dma((2, NX)),
-            dma((2, NX)),
-        ],
+            dma((LAYERS, 2)),
+        ]
+        + [dma((2,))] * 2
+        + [dma((NX,))] * 4
+        + [dma((2, NX))] * 12,
         compiler_params=pltpu.CompilerParams(
             collective_id=0, has_side_effects=True, vmem_limit_bytes=60 * 1024 * 1024
         ),

time: 154 us -> 149 us (0.968)
  Pallas kernels: 152 us -> 147 us
    pallas_call x1, Pallas kernels: 152 us -> 147 us  [per_device(): pl.pallas_call(stack_kernel, out_shape=jax.ShapeDtypeStruct((2, 32, 1024)...]
where the time goes in v5:
time: 149 us
  Pallas kernels  147 us (99%)
  local copies, waits for them, and re-layouts  1.57 us (1%)
    pallas_call x1, Pallas kernels, per_device(): pl.pallas_call(stack_kernel, out_shape=jax.ShapeDtypeStruct((2, 32, 1024)...  147 us

profile of v5, /device:TPU:1, one launch (start us, length us, event | category | flops | bytes accessed | tf_op | source)
XLA Modules:
  0.0 148.5 jit_solution(8125771841933895485)
XLA Ops:
  0.0 147.0 %shard_map.109 = bf16[2,32,1024]{2,1,0:T(8,128)(2,1)} custom-call(s32[1,2]{1,0:T(1,128)} %order.1, s32[2]{0:T(128)} %boundary.1, s32[2]{0:T(128)} %offset.1, s32[2,4]{1,0:T(2,128)} %lengths.1, bf16[2,64,1024]{2,1,0:T(8,128)(2,1)} %tokens.1, f32[8,128]{1,0:T(8,128)} %constant.2.clone.freq, f32[2,1,4096]{2,1,0:T(1,128)} %gain_in.1, ...), custom_call_target="tpu_custom_call" | custom-call | tf_op jit(solution)/shard_map/pallas_call | solution.py:703
  147.0 1.6 %copy.13 = bf16[2,32,1024]{2,1,0:T(8,128)(2,1)} copy(bf16[2,32,1024]{2,1,0:T(8,128)(2,1)} %shard_map.109) | data formatting | bytes 262144

commit v6 on v5

--- a/solution.py
+++ b/solution.py
@@ -231,6 +231,7 @@
         return wob.at[c, pl.ds(pl.multiple_of(k * rows, rows), rows), rows_of(zz)]
 
     hop_r = (hop_rq, hop_ro)
+
     own_r = (own_rq, own_ro)
 
     def whole(c, zz, t):
@@ -291,15 +292,19 @@
         ref = stretch(c, t)
         remote(ref, ref, par_s.at[t], par_r.at[c, t], other).wait_recv()
 
-    def load_and_share(d):
-        for t in range(2):
-            landed = whole(layer_of(d), z, t)
-            pltpu.make_async_copy(landed, landed, lsem.at[d, t]).wait()
-            for j in range(PIECES[t]):
-                own_swap(layer_of(d), t, nth(t, j, 1 - p)).start()
-
-    load_and_share(0)
+    def loaded(d, t):
+        landed = whole(layer_of(d), z, t)
+        pltpu.make_async_copy(landed, landed, lsem.at[d, t]).wait()
+
+    def share(d, t):
+        for j in range(PIECES[t]):
+            own_swap(layer_of(d), t, nth(t, j, 1 - p)).start()
+
+    loaded(0, 0)
+    share(0, 0)
     first_hop(0, 0)
+    loaded(0, 1)
+    share(0, 1)
 
     def run(event):
         c, t, h = event
@@ -330,13 +335,13 @@
     def tok_out(i):
         xx = (x + i) % NX
         return remote(
-            tsend.at[xx], block(xbuf.at[0, y], x, SEQ), t_s.at[xx], t_r.at[x], at(z, xx, p, y)
+            tsend.at[xx], block(xbuf.at[0, y], x, SEQ), t_s.at[0], t_r.at[x], at(z, xx, p, y)
         )
 
     def tok_in(i):
         xx = (x + i) % NX
         return remote(
-            tsend.at[xx], block(xbuf.at[0, y], xx, SEQ), t_s.at[xx], t_r.at[xx], at(z, xx, p, y)
+            tsend.at[xx], block(xbuf.at[0, y], xx, SEQ), t_s.at[0], t_r.at[xx], at(z, xx, p, y)
         )
 
     for i in (2, 1, 3):
@@ -344,7 +349,9 @@
     xbuf[0, y, pl.ds(pl.multiple_of(x * SEQ, SEQ), SEQ), :] = tsend[x]
 
     forward(0, 0, 1)
-    load_and_share(1)
+    for t in range(2):
+        loaded(1, t)
+        share(1, t)
 
     for d in range(2):
         c = layer_of(d)
@@ -353,7 +360,7 @@
             gbuf[c, :, zz * CHUNK : zz * CHUNK + CHUNK] = jnp.broadcast_to(row, (8, CHUNK))
 
     def gain_swap(d, c):
-        return remote(gbuf.at[c], gbuf.at[c], g_s.at[d], g_r.at[d], other)
+        return remote(gbuf.at[c], gbuf.at[c], g_s.at[0], g_r.at[d], other)
 
     for d in range(2):
         gain_swap(d, layer_of(d)).start()
@@ -364,12 +371,12 @@
     def stream_out(c, st, i):
         yy = (y + i) % NY
         ref = xbuf.at[c, y, stream_rows(st), :]
-        return remote(ref, ref, x_s.at[st, yy], x_r.at[st, y], at(z, x, p, yy))
+        return remote(ref, ref, x_s.at[st], x_r.at[st, y], at(z, x, p, yy))
 
     def stream_in(c, st, i):
         yy = (y + i) % NY
         ref = xbuf.at[c, yy, stream_rows(st), :]
-        return remote(ref, ref, x_s.at[st, yy], x_r.at[st, yy], at(z, x, p, yy))
+        return remote(ref, ref, x_s.at[st], x_r.at[st, yy], at(z, x, p, yy))
 
     for i in (2, 1, 3):
         tok_in(i).wait_recv()
@@ -397,11 +404,11 @@
 
     def table_out(i):
         xx = (x + i) % NX
-        return remote(tables.at[x], tables.at[x], tab_s.at[xx], tab_r.at[x], at(z, xx, p, y))
+        return remote(tables.at[x], tables.at[x], tab_s.at[0], tab_r.at[x], at(z, xx, p, y))
 
     def table_in(i):
         xx = (x + i) % NX
-        return remote(tables.at[xx], tables.at[xx], tab_s.at[xx], tab_r.at[xx], at(z, xx, p, y))
+        return remote(tables.at[xx], tables.at[xx], tab_s.at[0], tab_r.at[xx], at(z, xx, p, y))
 
     for i in (2, 1, 3):
         table_out(i).start()
@@ -419,7 +426,7 @@
         return remote(
             psend.at[st, xx],
             precv.at[c, st, x],
-            p_s.at[st, xx],
+            p_s.at[st],
             p_r.at[st, x],
             at(z, xx, p, y),
         )
@@ -429,7 +436,7 @@
         return remote(
             psend.at[st, xx],
             precv.at[c, st, xx],
-            p_s.at[st, xx],
+            p_s.at[st],
             p_r.at[st, xx],
             at(z, xx, p, y),
         )
@@ -439,7 +446,7 @@
         return remote(
             qsend.at[st, xx // 2],
             qrecv.at[c, st, x],
-            q_s.at[st, xx],
+            q_s.at[st],
             q_r.at[st, x],
             at(z, xx, p, y),
         )
@@ -449,42 +456,41 @@
         return remote(
             qsend.at[st, xx // 2],
             qrecv.at[c, st, xx],
-            q_s.at[st, xx],
+            q_s.at[st],
             q_r.at[st, xx],
             at(z, xx, p, y),
         )
 
+    def sent(ref, sem):
+        pltpu.make_async_copy(ref, ref, sem).wait()
+
     def attn_ref(c, st, xx):
         return abuf.at[c, st, xx % 2, xx // 2]
 
     def attn_out(c, st, i):
         xx = (x + i) % NX
         ref = attn_ref(c, st, x)
-        return remote(ref, ref, a_s.at[st, xx], a_r.at[st, x], at(z, xx, p, y))
+        return remote(ref, ref, a_s.at[st], a_r.at[st, x], at(z, xx, p, y))
 
     def attn_in(c, st, i):
         xx = (x + i) % NX
         ref = attn_ref(c, st, xx)
-        return remote(ref, ref, a_s.at[st, xx], a_r.at[st, xx], at(z, xx, p, y))
+        return remote(ref, ref, a_s.at[st], a_r.at[st, xx], at(z, xx, p, y))
 
     def proj_out(c, st, yy):
         return remote(
-            osend.at[st, yy], orecv.at[c, st, y], o_s.at[st, yy], o_r.at[st, y], at(z, x, p, yy)
+            osend.at[st, yy], orecv.at[c, st, y], o_s.at[st], o_r.at[st, y], at(z, x, p, yy)
         )
 
     def proj_in(c, st, yy):
         return remote(
-            osend.at[st, yy], orecv.at[c, st, yy], o_s.at[st, yy], o_r.at[st, yy], at(z, x, p, yy)
+            osend.at[st, yy], orecv.at[c, st, yy], o_s.at[st], o_r.at[st, yy], at(z, x, p, yy)
         )
 
     def project_stage(c, st):
         for i in (1, 3, 2):
             attn_in(c, st, i).wait_recv()
-        for xx in range(NX):
-
-            @pl.when(xx != x)
-            def _():
-                part_out(c, st, xx).wait_send()
+        sent(psend.at[st, pl.ds(0, 3)], p_s.at[st])
 
         def proj(yy):
             cols = pl.ds(pl.multiple_of(yy * PIECE, PIECE), PIECE)
@@ -509,10 +515,9 @@
     def add_stage(c, st):
         for i in (1, 3, 2):
             proj_in(c, st, (y + i) % NY).wait_recv()
-        for i in (1, 2, 3):
-            proj_out(c, st, (y + i) % NY).wait_send()
-            attn_out(c, st, i).wait_send()
-            square_out(c, st, i).wait_send()
+        sent(osend.at[st, pl.ds(0, 3)], o_s.at[st])
+        sent(psend.at[st, pl.ds(0, 2)], a_s.at[st])
+        sent(qrecv.at[c, st, pl.ds(0, 3)], q_s.at[st])
         for b in range(2):
             rows = slice(b * SEQ, b * SEQ + SEQ)
             places = slice(st * STREAM + b * SEQ, st * STREAM + b * SEQ + SEQ)
@@ -580,8 +585,7 @@
         inv_rms = lax.rsqrt(square * (1.0 / WIDTH) + NORM_EPSILON)
         for i in (1, 3, 2):
             part_in(c, st, i).wait_recv()
-        for i in (1, 2, 3):
-            stream_out(c, st, i).wait_send()
+        sent(osend.at[st, pl.ds(0, 3)], x_s.at[st])
         mine = st * 2 + x // 2
 
         def summed(b):
@@ -614,6 +618,28 @@
         for i in (2, 1, 3):
             attn_out(c, st, i).start()
 
+    def done_rows(xx, q):
+        return pl.ds(pl.multiple_of(xx * SEQ + q * 32, 32), 32)
+
+    def hand_over(st):
+        for xx in (2 * st, 2 * st + 1):
+            for q in range(2):
+                here = (xx == x) & (q == p)
+
+                @pl.when(jnp.logical_not(here))
+                def _():
+                    remote(
+                        xbuf.at[LAYERS, y, done_rows(xx, q), :],
+                        frecv.at[p, x],
+                        f_s.at[0],
+                        f_r.at[p, x],
+                        at(z, xx, q, y),
+                    ).start()
+
+                @pl.when(here)
+                def _():
+                    frecv[p, x] = xbuf[LAYERS, y, done_rows(xx, q), :]
+
     stages = (qkv_stage, attention_stage, project_stage, add_stage)
 
     def layer(c, carry):
@@ -629,37 +655,27 @@
             if slot == 4:
                 ready(c, 1)
             stages[slot // 2](c, slot % 2)
+            if slot >= 6:
+
+                @pl.when(c == LAYERS - 1)
+                def _():
+                    hand_over(slot - 6)
+
         return carry
 
     lax.fori_loop(0, LAYERS, layer, 0)
-
-    def done_rows(xx, q):
-        return pl.ds(pl.multiple_of(xx * SEQ + q * 32, 32), 32)
-
-    def done_out(i, j):
-        xx, q = (x + i) % NX, (p + j) % 2
-        return remote(
-            xbuf.at[LAYERS, y, done_rows(xx, q), :],
-            frecv.at[p, x],
-            f_s.at[q, xx],
-            f_r.at[p, x],
-            at(z, xx, q, y),
-        )
 
     def done_in(i, j):
         xx, q = (x + i) % NX, (p + j) % 2
         return remote(
             xbuf.at[LAYERS, y, done_rows(xx, q), :],
             frecv.at[q, xx],
-            f_s.at[q, xx],
+            f_s.at[0],
             f_r.at[q, xx],
             at(z, xx, q, y),
         )
 
     away = [(i, j) for i in (2, 1, 3, 0) for j in range(2) if (i, j) != (0, 0)]
-    for i, j in away:
-        done_out(i, j).start()
-    frecv[p, x] = xbuf[LAYERS, y, done_rows(x, p), :]
     for i, j in away:
         done_in(i, j).wait_recv()
     for q in range(2):
@@ -667,14 +683,10 @@
             out[q, :, xx * 128 : xx * 128 + 128] = frecv[q, xx, :, 0:128]
             out[q, :, 512 + xx * 128 : 512 + xx * 128 + 128] = frecv[q, xx, :, 128:256]
 
-    for i, j in away:
-        done_out(i, j).wait_send()
-    for i in (1, 2, 3):
-        tok_out(i).wait_send()
-        table_out(i).wait_send()
-    for d in range(2):
-        gain_swap(d, layer_of(d)).wait_send()
-
+    sent(xbuf.at[LAYERS, 0, pl.ds(0, 224), :], f_s.at[0])
+    sent(tsend.at[pl.ds(0, 3)], t_s.at[0])
+    sent(tables.at[pl.ds(0, 3)], tab_s.at[0])
+    sent(gbuf.at[pl.ds(0, 2)], g_s.at[0])
     for t in range(2):
         ref = wqkv.at[0, pl.ds(0, 256), :] if t == 0 else wob.at[0, pl.ds(0, 256), :]
         remote(ref, ref, own_s.at[t], own_r[t].at[0, 0], other).wait_send()
@@ -736,9 +748,10 @@
             dma((2,)),
             dma((LAYERS, 2)),
         ]
-        + [dma((2,))] * 2
-        + [dma((NX,))] * 4
-        + [dma((2, NX))] * 12,
+        + [dma((1,)), dma((2,))]
+        + [dma((1,)), dma((NX,))] * 2
+        + [dma((2,)), dma((2, NX))] * 5
+        + [dma((1,)), dma((2, NX))],
         compiler_params=pltpu.CompilerParams(
             collective_id=0, has_side_effects=True, vmem_limit_bytes=60 * 1024 * 1024
         ),

time: 149 us -> 147 us (0.987)
  Pallas kernels: 147 us -> 145 us
    pallas_call x1, Pallas kernels: 147 us -> 145 us  [per_device(): pl.pallas_call(stack_kernel, out_shape=jax.ShapeDtypeStruct((2, 32, 1024)...]
where the time goes in v6:
time: 147 us
  Pallas kernels  145 us (99%)
  local copies, waits for them, and re-layouts  1.57 us (1%)
    pallas_call x1, Pallas kernels, per_device(): pl.pallas_call(stack_kernel, out_shape=jax.ShapeDtypeStruct((2, 32, 1024)...  145 us

profile of v6, /device:TPU:1, one launch (start us, length us, event | category | flops | bytes accessed | tf_op | source)
XLA Modules:
  0.0 146.6 jit_solution(14870722671449078959)
XLA Ops:
  0.0 145.0 %shard_map.109 = bf16[2,32,1024]{2,1,0:T(8,128)(2,1)} custom-call(s32[1,2]{1,0:T(1,128)} %order.1, s32[2]{0:T(128)} %boundary.1, s32[2]{0:T(128)} %offset.1, s32[2,4]{1,0:T(2,128)} %lengths.1, bf16[2,64,1024]{2,1,0:T(8,128)(2,1)} %tokens.1, f32[8,128]{1,0:T(8,128)} %constant.2.clone.freq, f32[2,1,4096]{2,1,0:T(1,128)} %gain_in.1, ...), custom_call_target="tpu_custom_call" | custom-call | tf_op jit(solution)/shard_map/pallas_call | solution.py:715
  145.0 1.6 %copy.13 = bf16[2,32,1024]{2,1,0:T(8,128)(2,1)} copy(bf16[2,32,1024]{2,1,0:T(8,128)(2,1)} %shard_map.109) | data formatting | bytes 262144

commit v7 on v6

--- a/solution.py
+++ b/solution.py
@@ -56,44 +56,44 @@
     return rest * series(SINE_TERMS, square), series(COSINE_TERMS, square)
 
 
-PROLOGUE = ((0, 1, 0), (0, 1, 1), (0, 0, 4), (1, 0, 0))
+PROLOGUE = ((0, 0, 2), (0, 1, 0), (0, 0, 3), (0, 1, 1), (1, 0, 0), (0, 0, 4))
 EVENTS = (
     (
         (),
         ((0, 1, 2),),
-        ((1, 0, 1), (0, 1, 3)),
-        (),
-        ((1, 0, 2), (1, 1, 0), (0, 1, 4)),
-        (),
-        ((1, 0, 3), (1, 1, 1)),
-        ((2, 0, 0), (1, 0, 4)),
+        ((1, 0, 1),),
+        ((0, 1, 3), (1, 1, 0)),
+        ((1, 0, 2), (0, 1, 4)),
+        ((1, 1, 1),),
+        ((1, 0, 3), (2, 1, 0)),
+        (),
     ),
     (
-        ((1, 1, 2),),
-        ((2, 0, 1),),
-        (),
-        ((1, 1, 3), (2, 1, 0)),
-        ((1, 1, 4), (2, 0, 2)),
-        (),
-        ((2, 0, 3), (2, 1, 1)),
-        ((3, 0, 0), (2, 0, 4)),
+        ((1, 0, 4), (1, 1, 2), (2, 0, 0)),
+        (),
+        ((1, 1, 3), (2, 0, 1)),
+        (),
+        ((1, 1, 4), (2, 0, 2), (2, 1, 1)),
+        (),
+        ((2, 0, 3),),
+        ((2, 1, 2),),
     ),
     (
-        (),
-        ((2, 1, 2),),
-        ((3, 1, 0), (2, 1, 3), (3, 0, 1)),
-        (),
-        ((2, 1, 4),),
+        ((3, 0, 0), (2, 0, 4)),
+        ((2, 1, 3),),
+        ((2, 1, 4), (3, 0, 1), (3, 1, 0)),
+        (),
         ((3, 0, 2),),
-        (),
-        ((3, 0, 3), (3, 1, 1)),
+        ((3, 1, 1),),
+        ((3, 0, 3),),
+        ((3, 1, 2),),
     ),
     (
         ((3, 0, 4),),
-        ((3, 1, 2),),
+        (),
         ((3, 1, 3),),
+        (),
         ((3, 1, 4),),
-        (),
         (),
         (),
         (),
@@ -128,7 +128,6 @@
     osend,
     oown,
     orecv,
-    frecv,
     tok_v,
     freq_v,
     gain,
@@ -413,8 +412,6 @@
     for i in (2, 1, 3):
         table_out(i).start()
 
-    forward(0, 0, 2)
-    forward(0, 0, 3)
     for event in PROLOGUE:
         run(event)
     for d in range(2):
@@ -626,19 +623,18 @@
             for q in range(2):
                 here = (xx == x) & (q == p)
 
-                @pl.when(jnp.logical_not(here))
-                def _():
-                    remote(
-                        xbuf.at[LAYERS, y, done_rows(xx, q), :],
-                        frecv.at[p, x],
-                        f_s.at[0],
-                        f_r.at[p, x],
-                        at(z, xx, q, y),
-                    ).start()
-
-                @pl.when(here)
-                def _():
-                    frecv[p, x] = xbuf[LAYERS, y, done_rows(xx, q), :]
+                for half in range(2):
+                    rows = xbuf.at[LAYERS, y, done_rows(xx, q), pl.ds(half * 128, 128)]
+                    first = pl.multiple_of(half * 512 + x * 128, 128)
+                    place = out.at[p, :, pl.ds(first, 128)]
+
+                    @pl.when(jnp.logical_not(here))
+                    def _():
+                        remote(rows, place, f_s.at[0], f_r.at[p, x], at(z, xx, q, y)).start()
+
+                    @pl.when(here)
+                    def _():
+                        pltpu.make_async_copy(rows, place, isem.at[0]).start()
 
     stages = (qkv_stage, attention_stage, project_stage, add_stage)
 
@@ -665,23 +661,11 @@
 
     lax.fori_loop(0, LAYERS, layer, 0)
 
-    def done_in(i, j):
-        xx, q = (x + i) % NX, (p + j) % 2
-        return remote(
-            xbuf.at[LAYERS, y, done_rows(xx, q), :],
-            frecv.at[q, xx],
-            f_s.at[0],
-            f_r.at[q, xx],
-            at(z, xx, q, y),
-        )
-
     away = [(i, j) for i in (2, 1, 3, 0) for j in range(2) if (i, j) != (0, 0)]
+    landed = xbuf.at[LAYERS, y, done_rows(0, 0), :]
     for i, j in away:
-        done_in(i, j).wait_recv()
-    for q in range(2):
-        for xx in range(NX):
-            out[q, :, xx * 128 : xx * 128 + 128] = frecv[q, xx, :, 0:128]
-            out[q, :, 512 + xx * 128 : 512 + xx * 128 + 128] = frecv[q, xx, :, 128:256]
+        sent(landed, f_r.at[(p + j) % 2, (x + i) % NX])
+    sent(landed, isem.at[0])
 
     sent(xbuf.at[LAYERS, 0, pl.ds(0, 224), :], f_s.at[0])
     sent(tsend.at[pl.ds(0, 3)], t_s.at[0])
@@ -707,7 +691,6 @@
     doc_lengths,
     batch_order,
 ):
-    vmem = pl.BlockSpec(memory_space=pltpu.VMEM)
     smem = pl.BlockSpec(memory_space=pltpu.SMEM)
     anywhere = pl.BlockSpec(memory_space=pl.ANY)
     dma = pltpu.SemaphoreType.DMA
@@ -716,7 +699,7 @@
         stack_kernel,
         out_shape=jax.ShapeDtypeStruct((2, 32, 1024), bf16),
         in_specs=[smem] * 4 + [anywhere] * 7,
-        out_specs=vmem,
+        out_specs=anywhere,
         scratch_shapes=[
             pltpu.VMEM((LAYERS, SET, QKV), bf16),
             pltpu.VMEM((LAYERS, HEADS, SET), bf16),
@@ -732,7 +715,6 @@
             pltpu.VMEM((2, NY, STREAM, PIECE), bf16),
             pltpu.VMEM((2, STREAM, PIECE), f32),
             pltpu.VMEM((LAYERS, 2, NY, STREAM, PIECE), bf16),
-            pltpu.VMEM((2, NX, 32, PIECE), bf16),
             pltpu.VMEM((2, SEQ, 1024), bf16),
             pltpu.VMEM((8, HEAD_DIM), f32),
             pltpu.VMEM((2, 1, WIDTH), f32),

time: 147 us -> 145 us (0.986)
  Pallas kernels: 145 us -> 143 us
    pallas_call x1, Pallas kernels: 145 us -> 143 us  [per_device(): pl.pallas_call(stack_kernel, out_shape=jax.ShapeDtypeStruct((2, 32, 1024)...]
where the time goes in v7:
time: 145 us; the launch traced here: 144 us
  Pallas kernels  143 us (99%)
  local copies, waits for them, and re-layouts  1.57 us (1%)
    pallas_call x1, Pallas kernels, per_device(): pl.pallas_call(stack_kernel, out_shape=jax.ShapeDtypeStruct((2, 32, 1024)...  143 us

profile of v7, /device:TPU:1, one launch (start us, length us, event | category | flops | bytes accessed | tf_op | source)
XLA Modules:
  0.0 144.4 jit_solution(16022596996309640353)
XLA Ops:
  0.0 142.8 %shard_map.109 = bf16[2,32,1024]{2,1,0:T(8,128)(2,1)} custom-call(s32[1,2]{1,0:T(1,128)} %order.1, s32[2]{0:T(128)} %boundary.1, s32[2]{0:T(128)} %offset.1, s32[2,4]{1,0:T(2,128)} %lengths.1, bf16[2,64,1024]{2,1,0:T(8,128)(2,1)} %tokens.1, f32[8,128]{1,0:T(8,128)} %constant.2.clone.freq, f32[2,1,4096]{2,1,0:T(1,128)} %gain_in.1, ...), custom_call_target="tpu_custom_call" | custom-call | tf_op jit(solution)/shard_map/pallas_call | solution.py:698
  142.8 1.6 %copy.13 = bf16[2,32,1024]{2,1,0:T(8,128)(2,1)} copy(bf16[2,32,1024]{2,1,0:T(8,128)(2,1)} %shard_map.109) | data formatting | bytes 262144

commit v8 on v7

--- a/solution.py
+++ b/solution.py
@@ -343,7 +343,7 @@
             tsend.at[xx], block(xbuf.at[0, y], xx, SEQ), t_s.at[0], t_r.at[xx], at(z, xx, p, y)
         )
 
-    for i in (2, 1, 3):
+    for i in (1, 3, 2):
         tok_out(i).start()
     xbuf[0, y, pl.ds(pl.multiple_of(x * SEQ, SEQ), SEQ), :] = tsend[x]
 
@@ -377,10 +377,10 @@
         ref = xbuf.at[c, yy, stream_rows(st), :]
         return remote(ref, ref, x_s.at[st], x_r.at[st, yy], at(z, x, p, yy))
 
-    for i in (2, 1, 3):
+    for i in (1, 3, 2):
         tok_in(i).wait_recv()
     for st in range(2):
-        for i in (2, 1, 3):
+        for i in (1, 3, 2):
             stream_out(0, st, i).start()
 
     row = lax.broadcasted_iota(jnp.int32, (SEQ, 128), 0)
@@ -409,14 +409,14 @@
         xx = (x + i) % NX
         return remote(tables.at[xx], tables.at[xx], tab_s.at[0], tab_r.at[xx], at(z, xx, p, y))
 
-    for i in (2, 1, 3):
+    for i in (1, 3, 2):
         table_out(i).start()
 
     for event in PROLOGUE:
         run(event)
     for d in range(2):
         gain_swap(d, 1 - p + d * (1 + 2 * p)).wait_recv()
-    for i in (2, 1, 3):
+    for i in (1, 3, 2):
         table_in(i).wait_recv()
 
     def part_out(c, st, xx):
@@ -526,7 +526,7 @@
 
         @pl.when(c < LAYERS - 1)
         def _():
-            for i in (2, 1, 3):
+            for i in (1, 3, 2):
                 stream_out(c + 1, st, i).start()
 
     def qkv_stage(c, st):
@@ -543,11 +543,12 @@
                 xg[yy, rows, :] = (wide * gains).astype(jnp.bfloat16)
             flat = jnp.sum(jnp.where(row == lane, total, 0.0), axis=0, keepdims=True)
             qsend[st, b] = jnp.broadcast_to(flat, (8, 128))
-        for i in (2, 1, 3):
+        for i in (1, 3, 2):
             square_out(c, st, i).start()
         if st == 0:
             ready(c, 0)
-        for g in range(2):
+        for turn in range(2):
+            g = (x + 1 + turn) % 2
 
             def qkv_tile(n, carry):
                 cols = pl.ds(pl.multiple_of(g * GROUP + n * 256, 256), 256)
@@ -612,7 +613,7 @@
         mixed = jnp.dot(weights, vals, preferred_element_type=jnp.float32).astype(jnp.bfloat16)
         for j in range(4):
             abuf[c, st, x % 2, x // 2, :, j * 128 : j * 128 + 128] = mixed[j * SEQ : j * SEQ + SEQ]
-        for i in (2, 1, 3):
+        for i in (1, 3, 2):
             attn_out(c, st, i).start()
 
     def done_rows(xx, q):

time: 145 us -> 143 us (0.986)
  Pallas kernels: 143 us -> 140 us
    pallas_call x1, Pallas kernels: 143 us -> 140 us  [per_device(): pl.pallas_call(stack_kernel, out_shape=jax.ShapeDtypeStruct((2, 32, 1024)...]
where the time goes in v8:
time: 143 us; the launch traced here: 141 us
  Pallas kernels  140 us (98%)
  local copies, waits for them, and re-layouts  1.57 us (1%)
    pallas_call x1, Pallas kernels, per_device(): pl.pallas_call(stack_kernel, out_shape=jax.ShapeDtypeStruct((2, 32, 1024)...  140 us

profile of v8, /device:TPU:1, one launch (start us, length us, event | category | flops | bytes accessed | tf_op | source)
XLA Modules:
  0.0 141.5 jit_solution(5295907534376120995)
XLA Ops:
  0.0 139.9 %shard_map.109 = bf16[2,32,1024]{2,1,0:T(8,128)(2,1)} custom-call(s32[1,2]{1,0:T(1,128)} %order.1, s32[2]{0:T(128)} %boundary.1, s32[2]{0:T(128)} %offset.1, s32[2,4]{1,0:T(2,128)} %lengths.1, bf16[2,64,1024]{2,1,0:T(8,128)(2,1)} %tokens.1, f32[8,128]{1,0:T(8,128)} %constant.2.clone.freq, f32[2,1,4096]{2,1,0:T(1,128)} %gain_in.1, ...), custom_call_target="tpu_custom_call" | custom-call | tf_op jit(solution)/shard_map/pallas_call | solution.py:699
  139.9 1.6 %copy.13 = bf16[2,32,1024]{2,1,0:T(8,128)(2,1)} copy(bf16[2,32,1024]{2,1,0:T(8,128)(2,1)} %shard_map.109) | data formatting | bytes 262144

commit v9 on v8

--- a/solution.py
+++ b/solution.py
@@ -501,12 +501,12 @@
             return total
 
         def proj_tile(i, carry):
-            yy = (y + i) % NY
+            yy = (y + 1 + (2 * i) % 3) % NY
             osend[st, yy] = proj(yy).astype(jnp.bfloat16)
             proj_out(c, st, yy).start()
             return carry
 
-        lax.fori_loop(1, NY, proj_tile, 0)
+        lax.fori_loop(0, NY - 1, proj_tile, 0)
         oown[st] = proj(y)
 
     def add_stage(c, st):

time: 143 us -> 143 us (level)
  no operation moved by 1% of the time
where the time goes in v9:
time: 143 us; the launch traced here: 142 us
  Pallas kernels  141 us (99%)
  local copies, waits for them, and re-layouts  1.57 us (1%)
    pallas_call x1, Pallas kernels, per_device(): pl.pallas_call(stack_kernel, out_shape=jax.ShapeDtypeStruct((2, 32, 1024)...  141 us

profile of v9, /device:TPU:1, one launch (start us, length us, event | category | flops | bytes accessed | tf_op | source)
XLA Modules:
  0.0 142.4 jit_solution(14802394768271540188)
XLA Ops:
  0.0 140.8 %shard_map.109 = bf16[2,32,1024]{2,1,0:T(8,128)(2,1)} custom-call(s32[1,2]{1,0:T(1,128)} %order.1, s32[2]{0:T(128)} %boundary.1, s32[2]{0:T(128)} %offset.1, s32[2,4]{1,0:T(2,128)} %lengths.1, bf16[2,64,1024]{2,1,0:T(8,128)(2,1)} %tokens.1, f32[8,128]{1,0:T(8,128)} %constant.2.clone.freq, f32[2,1,4096]{2,1,0:T(1,128)} %gain_in.1, ...), custom_call_target="tpu_custom_call" | custom-call | tf_op jit(solution)/shard_map/pallas_call | solution.py:699
  140.8 1.6 %copy.13 = bf16[2,32,1024]{2,1,0:T(8,128)(2,1)} copy(bf16[2,32,1024]{2,1,0:T(8,128)(2,1)} %shard_map.109) | data formatting | bytes 262144
